TPU v7x, 512 devices: a whole 4x8x8 slice. The times are simulated.
512 devices in a mesh: bins: 128 (over z, y, core), scans: 4 (over x).
Axes of the slice: x: 4, y: 8, z: 8, core: 2. Of those that a mesh axis runs over, the one named last changes fastest.
Arguments:
- profiles: float32 [4, 4194304], P('scans', 'bins'), may hold values from -150 to 150
- band_edges: int32 [6], replicated, may hold values from 0 to 4096, as said below
- owner_counts: int32 [128], replicated, may hold values from 1 to 64, 4096 in all
- dynamics: float32 [5, 64, 64], replicated, may hold values from -0.6 to 0.6
- prev_state: float32 [8192, 4, 128], P('bins', 'scans'), may hold values from -6 to 6
Outputs:
- new_state: float32 [8192, 4, 128], P('bins', 'scans')
Inputs may be any that keep to these rules, and one draw needn't show every extreme that they name: Strictly increasing, band_edges[0] = 0 and band_edges[5] = 4096. `owner_counts`: the counts sum to 4096, and some owner holds exactly 64 tiles.
All inputs are finite; a program needn't handle non-finite values.
Results may differ from a plain program's by a relative error of at most 0.0001.
Values sent between devices are 32-bit elements; how exact they have to be, the bound alone decides.
A program may use at most 64 MiB of HBM per device.

v0:
```python
import math

import jax
import jax.numpy as jnp
import numpy as np
from jax import lax
from jax.sharding import PartitionSpec as P

TILE = 512
STATES = 64
NCLASS = 5


EPSILON = 1e-05
HIGHEST = lax.Precision.HIGHEST


def swapped(shard, axis, apart):
    return lax.ppermute(shard, axis, [(i, i ^ 1 << apart) for i in range(lax.axis_size(axis))])


def reversed_bits(entry_count, levels):
    sources = np.arange(entry_count)
    flipped = np.zeros(entry_count, dtype=np.int64)
    for bit_number in range(levels):
        flipped = flipped | (sources >> bit_number & 1) << levels - 1 - bit_number
    return flipped.astype(np.int32)


def rotate(real_part, imag_part, angles):
    cosine_part = jnp.cos(angles)
    sine_part = jnp.sin(angles)
    return (
        real_part * cosine_part + imag_part * sine_part,
        imag_part * cosine_part - real_part * sine_part,
    )


def transform(pattern, cosine_part, sine_part, real_part, imag_part):
    real_out = jnp.einsum(pattern, cosine_part, real_part, precision=HIGHEST) + jnp.einsum(
        pattern, sine_part, imag_part, precision=HIGHEST
    )
    imag_out = jnp.einsum(pattern, cosine_part, imag_part, precision=HIGHEST) - jnp.einsum(
        pattern, sine_part, real_part, precision=HIGHEST
    )
    return (real_out, imag_out)


def measure(fine_sums, mean_power, band_index):
    measured = jnp.zeros_like(fine_sums)
    for class_index in range(NCLASS):
        group_span = 2**class_index
        state_count = STATES // group_span
        coarse = jnp.sum(
            fine_sums.reshape(fine_sums.shape[:-1] + (state_count, group_span)), axis=-1
        )
        coarse = jnp.pad(coarse, [(0, 0)] * (coarse.ndim - 1) + [(0, STATES - state_count)])
        scaling = 1.0 / jnp.sqrt(TILE // state_count * (mean_power + EPSILON))
        chosen = band_index == class_index
        measured = measured + jnp.where(
            chosen[:, None, None, None], coarse * scaling[:, None, None, None], 0.0
        )
    return measured


def update(dynamics, band_index, previous, measured, occupied):
    state_index = jnp.arange(STATES)
    blocks = []
    for class_index in range(NCLASS):
        state_count = STATES // 2**class_index
        inside = state_index < state_count
        blocks.append(jnp.where(inside[:, None] & inside[None, :], dynamics[class_index], 0.0))
    masked = jnp.stack(blocks)
    selection = (band_index[:, None] == jnp.arange(NCLASS)[None, :]).astype(masked.dtype)
    picked = jnp.einsum("rk,kij->rij", selection, masked, precision=HIGHEST)
    updated = jnp.einsum("rij,rpcj->rpci", picked, previous, precision=HIGHEST) + measured
    return jnp.where(occupied[:, None, None, None], updated, 0.0)


def owner_relay(values, powers):
    return (
        lax.all_to_all(values, "bins", split_axis=0, concat_axis=0, tiled=True),
        lax.all_to_all(powers, "bins", split_axis=0, concat_axis=0, tiled=True),
    )


def strided_owners(real_part, imag_part, source_residue, owner_counts, capacity):
    groups = lax.axis_size("bins")
    prof_rows, length = real_part.shape
    leading = 128
    trailing = length // leading
    retained = trailing // 2
    lead_index = jnp.arange(leading, dtype=jnp.int32)
    trail_index = jnp.arange(trailing, dtype=jnp.int32)
    keep_index = jnp.arange(retained, dtype=jnp.int32)
    angle_one = (
        2.0
        * math.pi
        * (lead_index[:, None] * lead_index[None, :] % leading).astype(jnp.float32)
        / leading
    )
    grid_real = real_part.reshape(prof_rows, leading, trailing)
    grid_imag = imag_part.reshape(prof_rows, leading, trailing)
    step_real, step_imag = transform(
        "bk,pkn->pbn", jnp.cos(angle_one), jnp.sin(angle_one), grid_real, grid_imag
    )
    angle_two = (
        2.0
        * math.pi
        * (lead_index[:, None] * trail_index[None, :] % length).astype(jnp.float32)
        / length
    )
    step_real, step_imag = rotate(step_real, step_imag, angle_two[None, :, :])
    angle_three = (
        2.0
        * math.pi
        * (trail_index[:, None] * keep_index[None, :] % trailing).astype(jnp.float32)
        / trailing
    )
    out_real, out_imag = transform(
        "nc,pbn->cbp", jnp.cos(angle_three), jnp.sin(angle_three), step_real, step_imag
    )
    share_bins = TILE // groups
    tile_count = retained * leading // share_bins
    payload = jnp.stack(
        [
            out_real.reshape(tile_count, share_bins, prof_rows),
            out_imag.reshape(tile_count, share_bins, prof_rows),
        ],
        axis=1,
    )
    payload = payload.reshape(tile_count, 2 * share_bins * prof_rows)
    starts = jnp.cumsum(owner_counts) - owner_counts
    slot_index = jnp.arange(capacity, dtype=jnp.int32)
    wanted = starts[:, None] + slot_index[None, :]
    filled = slot_index[None, :] < owner_counts[:, None]
    chosen = jnp.clip(wanted, 0, tile_count - 1)
    buffer = jnp.where(filled[:, :, None], payload[chosen], 0.0)
    piece_power = jnp.sum(buffer * buffer, axis=2)
    arrived, arrived_power = owner_relay(buffer, piece_power)
    arrived = arrived.reshape(groups, capacity, 2, share_bins, prof_rows)
    sub_width = TILE // STATES
    offsets = (
        groups * jnp.arange(share_bins, dtype=jnp.int32)[None, :]
        + jnp.asarray(source_residue)[:, None]
    )
    selector = (
        offsets[:, :, None] // sub_width == jnp.arange(STATES, dtype=jnp.int32)[None, None, :]
    ).astype(jnp.float32)
    fine_sums = jnp.einsum("drcjp,dji->rpci", arrived, selector, precision=HIGHEST)
    partial_power = jnp.sum(arrived_power, axis=0)
    return (fine_sums, partial_power)


def body(profiles, band_edges, owner_counts, dynamics, prev_state):
    groups = lax.axis_size("bins")
    levels = groups.bit_length() - 1
    own_index = lax.axis_index("bins")
    prof_rows, length = profiles.shape
    full_length = length * groups
    capacity = prev_state.shape[0]
    top_bit = levels - 1
    partner = swapped(profiles, "bins", top_bit)
    upper_half = own_index >> top_bit & 1 == 1
    angles = math.pi * (own_index % 2**top_bit).astype(jnp.float32) / 2**top_bit
    differ = partner - profiles
    real_part = jnp.where(upper_half, differ * jnp.cos(angles), profiles + partner)
    imag_part = jnp.where(upper_half, -differ * jnp.sin(angles), jnp.zeros_like(profiles))
    for bit_number in range(levels - 2, -1, -1):
        partner_real, partner_imag = swapped((real_part, imag_part), "bins", bit_number)
        upper_half = own_index >> bit_number & 1 == 1
        half_span = 2**bit_number
        angles = math.pi * (own_index % half_span).astype(jnp.float32) / half_span
        turned_real, turned_imag = rotate(
            partner_real - real_part, partner_imag - imag_part, angles
        )
        summed_real = real_part + partner_real
        summed_imag = imag_part + partner_imag
        real_part = jnp.where(upper_half, turned_real, summed_real)
        imag_part = jnp.where(upper_half, turned_imag, summed_imag)
    source_residue = reversed_bits(groups, levels)
    residue = jnp.asarray(source_residue)[own_index]
    positions = jnp.arange(length, dtype=jnp.int32)
    angles = 2.0 * math.pi * (positions * residue % full_length).astype(jnp.float32) / full_length
    real_part, imag_part = rotate(real_part, imag_part, angles[None, :])
    fine_sums, partial_power = strided_owners(
        real_part, imag_part, source_residue, owner_counts, capacity
    )
    summed_power = lax.psum(partial_power, "scans")
    mean_power = summed_power / (prof_rows * lax.axis_size("scans") * TILE)
    starts = jnp.cumsum(owner_counts) - owner_counts
    slot_index = jnp.arange(capacity, dtype=jnp.int32)
    own_start = starts[own_index]
    own_count = owner_counts[own_index]
    tile_ids = own_start + slot_index
    band_index = jnp.sum(
        (tile_ids[:, None] >= band_edges[None, 1:NCLASS]).astype(jnp.int32), axis=1
    )
    measured = measure(fine_sums, mean_power, band_index)
    previous = prev_state.reshape(capacity, prof_rows, 2, STATES)
    occupied = slot_index < own_count
    updated = update(dynamics, band_index, previous, measured, occupied)
    return updated.reshape(capacity, prof_rows, 2 * STATES)


def solution(mesh):
    return jax.shard_map(
        body,
        mesh=mesh,
        in_specs=(P("scans", "bins"), P(), P(), P(), P("bins", "scans", None)),
        out_specs=P("bins", "scans", None),
        check_vma=False,
    )
```

profile of v0, /device:TPU:1, one launch (start us, length us, event | category | flops | bytes accessed | tf_op | source)
XLA Modules:
  0.0 202.1 jit_solution(12722311403166517999)
XLA Ops:
  0.0 11.5 %collective-permute-start = (f32[1,32768]{1,0:T(1,128)}, f32[1,32768]{1,0:T(1,128)S(1)}, u32[]{:S(2)}, u32[]{:S(2)}) collective-permute-start(f32[1,32768]{1,0:T(1,128)} %param.6), channel_id=1, source_target_pairs={{0,256},{4,260},{8,264},{12,268},{16,272},{20,276},{24,280},{28,28... | collective-permute-start | bytes 393224 | tf_op jit(solution)/shard_map/ppermute | solution.py:19
  16.8 6.8 %collective-permute-start.1 = (f32[1,32768]{1,0:T(1,128)S(1)}, f32[1,32768]{1,0:T(1,128)S(1)}, u32[]{:S(2)}, u32[]{:S(2)}) collective-permute-start(f32[1,32768]{1,0:T(1,128)S(1)} %get-tuple-element.22), channel_id=1, source_target_pairs={{0,128},{4,132},{8,136},{12,140},{16,144},{20,148},{24,152},{28,15... | collective-permute-start | bytes 393224 | tf_op jit(solution)/shard_map/ppermute | solution.py:19
  26.9 5.8 %collective-permute-done.1 = f32[1,32768]{1,0:T(1,128)S(1)} collective-permute-done((f32[1,32768]{1,0:T(1,128)S(1)}, f32[1,32768]{1,0:T(1,128)S(1)}, u32[]{:S(2)}, u32[]{:S(2)}) %collective-permute-start.1) | collective-permute-done | bytes 131104 | tf_op jit(solution)/shard_map/ppermute | solution.py:19
  32.8 2.8 %collective-permute-done.2 = f32[1,32768]{1,0:T(1,128)S(1)} collective-permute-done((f32[1,32768]{1,0:T(1,128)S(1)}, f32[1,32768]{1,0:T(1,128)S(1)}, u32[]{:S(2)}, u32[]{:S(2)}) %collective-permute-start.2) | collective-permute-done | bytes 131104 | tf_op jit(solution)/shard_map/ppermute | solution.py:19
  37.9 3.4 %collective-permute-start.4 = (f32[1,32768]{1,0:T(1,128)S(1)}, f32[1,32768]{1,0:T(1,128)S(1)}, u32[]{:S(2)}, u32[]{:S(2)}) collective-permute-start(f32[1,32768]{1,0:T(1,128)S(1)} %get-tuple-element.19), channel_id=1, source_target_pairs={{0,64},{4,68},{8,72},{12,76},{16,80},{20,84},{24,88},{28,92},{32,9... | collective-permute-start | bytes 393224 | tf_op jit(solution)/shard_map/ppermute | solution.py:19
  41.7 3.6 %collective-permute-done.4 = f32[1,32768]{1,0:T(1,128)S(1)} collective-permute-done((f32[1,32768]{1,0:T(1,128)S(1)}, f32[1,32768]{1,0:T(1,128)S(1)}, u32[]{:S(2)}, u32[]{:S(2)}) %collective-permute-start.4) | collective-permute-done | bytes 131104 | tf_op jit(solution)/shard_map/ppermute | solution.py:19
  45.7 7.5 %collective-permute-start.5 = (f32[1,32768]{1,0:T(1,128)S(1)}, f32[1,32768]{1,0:T(1,128)S(1)}, u32[]{:S(2)}, u32[]{:S(2)}) collective-permute-start(f32[1,32768]{1,0:T(1,128)S(1)} %get-tuple-element.18), channel_id=1, source_target_pairs={{0,32},{4,36},{8,40},{12,44},{16,48},{20,52},{24,56},{28,60},{32,0... | collective-permute-start | bytes 393224 | tf_op jit(solution)/shard_map/ppermute | solution.py:19
  55.6 12.0 %collective-permute-done.6 = f32[1,32768]{1,0:T(1,128)S(1)} collective-permute-done((f32[1,32768]{1,0:T(1,128)S(1)}, f32[1,32768]{1,0:T(1,128)S(1)}, u32[]{:S(2)}, u32[]{:S(2)}) %collective-permute-start.6) | collective-permute-done | bytes 131104 | tf_op jit(solution)/shard_map/ppermute | solution.py:19
  70.0 4.3 %collective-permute-start.8 = (f32[1,32768]{1,0:T(1,128)S(1)}, f32[1,32768]{1,0:T(1,128)S(1)}, u32[]{:S(2)}, u32[]{:S(2)}) collective-permute-start(f32[1,32768]{1,0:T(1,128)S(1)} %get-tuple-element.15), channel_id=1, source_target_pairs={{0,16},{4,20},{8,24},{12,28},{16,0},{20,4},{24,8},{28,12},{32,48},... | collective-permute-start | bytes 393224 | tf_op jit(solution)/shard_map/ppermute | solution.py:19
  74.3 7.2 %collective-permute-done.7 = f32[1,32768]{1,0:T(1,128)S(1)} collective-permute-done((f32[1,32768]{1,0:T(1,128)S(1)}, f32[1,32768]{1,0:T(1,128)S(1)}, u32[]{:S(2)}, u32[]{:S(2)}) %collective-permute-start.7) | collective-permute-done | bytes 131104 | tf_op jit(solution)/shard_map/ppermute | solution.py:19
  81.5 2.8 %collective-permute-done.8 = f32[1,32768]{1,0:T(1,128)S(1)} collective-permute-done((f32[1,32768]{1,0:T(1,128)S(1)}, f32[1,32768]{1,0:T(1,128)S(1)}, u32[]{:S(2)}, u32[]{:S(2)}) %collective-permute-start.8) | collective-permute-done | bytes 131104 | tf_op jit(solution)/shard_map/ppermute | solution.py:19
  86.7 3.4 %collective-permute-start.9 = (f32[1,32768]{1,0:T(1,128)S(1)}, f32[1,32768]{1,0:T(1,128)S(1)}, u32[]{:S(2)}, u32[]{:S(2)}) collective-permute-start(f32[1,32768]{1,0:T(1,128)S(1)} %get-tuple-element.14), channel_id=1, source_target_pairs={{0,8},{4,12},{8,0},{12,4},{16,24},{20,28},{24,16},{28,20},{32,40},... | collective-permute-start | bytes 393224 | tf_op jit(solution)/shard_map/ppermute | solution.py:19
  94.5 3.2 %collective-permute-start.11 = (f32[1,32768]{1,0:T(1,128)S(1)}, f32[1,32768]{1,0:T(1,128)S(1)}, u32[]{:S(2)}, u32[]{:S(2)}) collective-permute-start(f32[1,32768]{1,0:T(1,128)S(1)} %get-tuple-element.12), channel_id=1, source_target_pairs={{0,4},{4,0},{8,12},{12,8},{16,20},{20,16},{24,28},{28,24},{32,36},... | collective-permute-start | bytes 393224 | tf_op jit(solution)/shard_map/ppermute | solution.py:19
  101.3 6.5 %subtract_reduce_fusion = (f32[32768]{0:T(1024)S(1)}, f32[32768]{0:T(1024)S(1)}) fusion(f32[1,32768]{1,0:T(1,128)S(1)} %get-tuple-element.10, f32[1,32768]{1,0:T(1,128)S(1)} %get-tuple-element.9, s32[]{:T(128)} %bitcast.12), kind=kLoop, calls=%fused_computation.63 | loop fusion | flops 655360 | bytes 524292 | tf_op jit(solution)/shard_map/sub | solution.py:35
  114.1 2.2 %stack_reshape.6 = f32[4096,1,4,1]{2,0,3,1:T(8,128)S(1)} reshape(f32[128,128,1]{1,0,2:T(8,128)S(1)} %copy.108) | data formatting | bytes 131072 | tf_op jit(solution)/shard_map/stack;reshape | solution.py:125
  118.3 2.2 %stack_reshape.7 = f32[4096,1,4,1]{2,0,3,1:T(8,128)S(1)} reshape(f32[128,128,1]{1,0,2:T(8,128)S(1)} %copy.109) | data formatting | bytes 131072 | tf_op jit(solution)/shard_map/stack;reshape | solution.py:125
  121.8 27.7 %gather_fusion = f32[8192,8]{1,0:T(8,128)} fusion(f32[4096,8]{1,0:T(8,128)S(1)} %copy.112, s32[8192]{0:T(1024)S(1)} %broadcast_clamp_fusion), kind=kCustom, calls=%fused_computation | custom fusion | bytes 557056 | tf_op jit(solution)/shard_map/gather | solution.py:138
  149.5 3.7 %copy.114 = f32[128,64,8]{0,2,1:T(8,128)S(1)} copy(f32[128,64,8]{2,1,0:T(8,128)} %bitcast.88) | data formatting | bytes 524288 | tf_op jit(solution)/shard_map/gather | solution.py:138
  154.0 6.3 %all-to-all-start.1 = ((f32[128,1,64]{2,1,0:T(1,128)}), f32[128,1,64]{2,1,0:T(1,128)S(1)}, u32[]{:S(2)}, u32[]{:S(2)}) async-start(f32[128,1,64]{2,1,0:T(1,128)} %copy.119), calls=%async_computation.1 | async-start | bytes 131072 | tf_op jit(solution)/shard_map/all_to_all | solution.py:83
  161.6 10.1 %all-to-all-done.1 = f32[128,1,64]{2,1,0:T(1,128)S(1)} async-done(((f32[128,1,64]{2,1,0:T(1,128)}), f32[128,1,64]{2,1,0:T(1,128)S(1)}, u32[]{:S(2)}, u32[]{:S(2)}) %all-to-all-start.1) | async-done | bytes 32800 | tf_op jit(solution)/shard_map/all_to_all | solution.py:83
  171.7 5.8 %all-to-all-start = ((f32[128,1,512]{2,1,0:T(1,128)}), f32[128,1,512]{2,1,0:T(1,128)S(1)}, u32[]{:S(2)}, u32[]{:S(2)}) async-start(f32[128,1,512]{2,1,0:T(1,128)} %reshape.711), calls=%async_computation | async-start | bytes 524288 | tf_op jit(solution)/shard_map/all_to_all | solution.py:82
  180.4 9.0 %psum.7 = f32[64]{0:T(128)S(1)} all-reduce(f32[64]{0:T(128)S(1)} %reduce_sum.77), channel_id=1, replica_groups=mesh['bins'=128,'scans'=4] {'scans'}, use_global_device_ids=true, to_apply=%region_4.5 | all-reduce | flops 64 | bytes 512 | tf_op jit(solution)/shard_map/psum | solution.py:189
  189.4 3.4 %all-to-all-done = f32[128,1,512]{2,1,0:T(1,128)S(1)} async-done(((f32[128,1,512]{2,1,0:T(1,128)}), f32[128,1,512]{2,1,0:T(1,128)S(1)}, u32[]{:S(2)}, u32[]{:S(2)}) %all-to-all-start) | async-done | bytes 262176 | tf_op jit(solution)/shard_map/all_to_all | solution.py:82
  196.1 5.2 %fusion.12 = f32[64,1,2,64]{3,2,0,1:T(2,128)S(1)} fusion(f32[64,2,64]{2,1,0:T(2,128)S(1)} %reshape.667, f32[64,64,64]{2,0,1:T(8,128)S(1)} %fusion.64, f32[64,1,2,4]{3,2,0,1:T(2,128)S(1)} %bitcast.105, f32[64,1,2,8]{3,2,0,1:T(2,128)S(1)} %bitcast.104, f32[64,1,2,16]{3,2,0,1:T(2,128)S(1)} %bitcast.102, f32[64,1,2,32]{3,2,0,1:T(2,128)S(1)} %bitcast.103, ...), kind=kOutput, calls=%fused_computation.14 | convolution fusion | flops 6422528 | bytes 1179264 | tf_op jit(solution)/shard_map/rij,rpcj->rpci/dot_general | solution.py:76
  (98 shorter events, 44.4 us)
Async XLA Ops:
  0.0 15.7 %collective-permute-start = (f32[1,32768]{1,0:T(1,128)}, f32[1,32768]{1,0:T(1,128)S(1)}, u32[]{:S(2)}, u32[]{:S(2)}) collective-permute-start(f32[1,32768]{1,0:T(1,128)} %param.6), channel_id=1, source_target_pairs={{0,256},{4,260},{8,264},{12,268},{16,272},{20,276},{24,280},{28,28... | collective-permute-start | bytes 393224 | tf_op jit(solution)/shard_map/ppermute | solution.py:19
  11.7 62.6 %copy-start.1 = (s32[128]{0:T(128)S(1)}, s32[128]{0:T(128)}, u32[]{:S(2)}) copy-start(s32[128]{0:T(128)} %param.8) | copy-start | bytes 1540
  14.7 76.8 %copy-start.2 = (s32[128]{0:T(128)S(1)}, s32[128]{0:T(128)}, u32[]{:S(2)}) copy-start(s32[128]{0:T(128)} %constant.243.clone) | copy-start | bytes 1540
  14.7 77.4 %copy-start.3 = (s32[6]{0:T(128)S(1)}, s32[6]{0:T(128)}, u32[]{:S(2)}) copy-start(s32[6]{0:T(128)} %param.7) | copy-start | bytes 76
  16.8 15.9 %collective-permute-start.1 = (f32[1,32768]{1,0:T(1,128)S(1)}, f32[1,32768]{1,0:T(1,128)S(1)}, u32[]{:S(2)}, u32[]{:S(2)}) collective-permute-start(f32[1,32768]{1,0:T(1,128)S(1)} %get-tuple-element.22), channel_id=1, source_target_pairs={{0,128},{4,132},{8,136},{12,140},{16,144},{20,148},{24,152},{28,15... | collective-permute-start | bytes 393224 | tf_op jit(solution)/shard_map/ppermute | solution.py:19
  23.6 12.0 %collective-permute-start.2 = (f32[1,32768]{1,0:T(1,128)S(1)}, f32[1,32768]{1,0:T(1,128)S(1)}, u32[]{:S(2)}, u32[]{:S(2)}) collective-permute-start(f32[1,32768]{1,0:T(1,128)S(1)} %get-tuple-element.21), channel_id=1, source_target_pairs={{0,128},{4,132},{8,136},{12,140},{16,144},{20,148},{24,152},{28,15... | collective-permute-start | bytes 393224 | tf_op jit(solution)/shard_map/ppermute | solution.py:19
  36.0 5.7 %collective-permute-start.3 = (f32[1,32768]{1,0:T(1,128)S(1)}, f32[1,32768]{1,0:T(1,128)S(1)}, u32[]{:S(2)}, u32[]{:S(2)}) collective-permute-start(f32[1,32768]{1,0:T(1,128)S(1)} %get-tuple-element.20), channel_id=1, source_target_pairs={{0,64},{4,68},{8,72},{12,76},{16,80},{20,84},{24,88},{28,92},{32,9... | collective-permute-start | bytes 393224 | tf_op jit(solution)/shard_map/ppermute | solution.py:19
  37.9 7.3 %collective-permute-start.4 = (f32[1,32768]{1,0:T(1,128)S(1)}, f32[1,32768]{1,0:T(1,128)S(1)}, u32[]{:S(2)}, u32[]{:S(2)}) collective-permute-start(f32[1,32768]{1,0:T(1,128)S(1)} %get-tuple-element.19), channel_id=1, source_target_pairs={{0,64},{4,68},{8,72},{12,76},{16,80},{20,84},{24,88},{28,92},{32,9... | collective-permute-start | bytes 393224 | tf_op jit(solution)/shard_map/ppermute | solution.py:19
  45.7 9.9 %collective-permute-start.5 = (f32[1,32768]{1,0:T(1,128)S(1)}, f32[1,32768]{1,0:T(1,128)S(1)}, u32[]{:S(2)}, u32[]{:S(2)}) collective-permute-start(f32[1,32768]{1,0:T(1,128)S(1)} %get-tuple-element.18), channel_id=1, source_target_pairs={{0,32},{4,36},{8,40},{12,44},{16,48},{20,52},{24,56},{28,60},{32,0... | collective-permute-start | bytes 393224 | tf_op jit(solution)/shard_map/ppermute | solution.py:19
  53.2 14.4 %collective-permute-start.6 = (f32[1,32768]{1,0:T(1,128)S(1)}, f32[1,32768]{1,0:T(1,128)S(1)}, u32[]{:S(2)}, u32[]{:S(2)}) collective-permute-start(f32[1,32768]{1,0:T(1,128)S(1)} %get-tuple-element.17), channel_id=1, source_target_pairs={{0,32},{4,36},{8,40},{12,44},{16,48},{20,52},{24,56},{28,60},{32,0... | collective-permute-start | bytes 393224 | tf_op jit(solution)/shard_map/ppermute | solution.py:19
  68.0 13.5 %collective-permute-start.7 = (f32[1,32768]{1,0:T(1,128)S(1)}, f32[1,32768]{1,0:T(1,128)S(1)}, u32[]{:S(2)}, u32[]{:S(2)}) collective-permute-start(f32[1,32768]{1,0:T(1,128)S(1)} %get-tuple-element.16), channel_id=1, source_target_pairs={{0,16},{4,20},{8,24},{12,28},{16,0},{20,4},{24,8},{28,12},{32,48},... | collective-permute-start | bytes 393224 | tf_op jit(solution)/shard_map/ppermute | solution.py:19
  70.0 14.3 %collective-permute-start.8 = (f32[1,32768]{1,0:T(1,128)S(1)}, f32[1,32768]{1,0:T(1,128)S(1)}, u32[]{:S(2)}, u32[]{:S(2)}) collective-permute-start(f32[1,32768]{1,0:T(1,128)S(1)} %get-tuple-element.15), channel_id=1, source_target_pairs={{0,16},{4,20},{8,24},{12,28},{16,0},{20,4},{24,8},{28,12},{32,48},... | collective-permute-start | bytes 393224 | tf_op jit(solution)/shard_map/ppermute | solution.py:19
  84.7 7.5 %collective-permute-start.10 = (f32[1,32768]{1,0:T(1,128)S(1)}, f32[1,32768]{1,0:T(1,128)S(1)}, u32[]{:S(2)}, u32[]{:S(2)}) collective-permute-start(f32[1,32768]{1,0:T(1,128)S(1)} %get-tuple-element.13), channel_id=1, source_target_pairs={{0,8},{4,12},{8,0},{12,4},{16,24},{20,28},{24,16},{28,20},{32,40},... | collective-permute-start | bytes 393224 | tf_op jit(solution)/shard_map/ppermute | solution.py:19
  86.7 7.4 %collective-permute-start.9 = (f32[1,32768]{1,0:T(1,128)S(1)}, f32[1,32768]{1,0:T(1,128)S(1)}, u32[]{:S(2)}, u32[]{:S(2)}) collective-permute-start(f32[1,32768]{1,0:T(1,128)S(1)} %get-tuple-element.14), channel_id=1, source_target_pairs={{0,8},{4,12},{8,0},{12,4},{16,24},{20,28},{24,16},{28,20},{32,40},... | collective-permute-start | bytes 393224 | tf_op jit(solution)/shard_map/ppermute | solution.py:19
  94.5 5.8 %collective-permute-start.11 = (f32[1,32768]{1,0:T(1,128)S(1)}, f32[1,32768]{1,0:T(1,128)S(1)}, u32[]{:S(2)}, u32[]{:S(2)}) collective-permute-start(f32[1,32768]{1,0:T(1,128)S(1)} %get-tuple-element.12), channel_id=1, source_target_pairs={{0,4},{4,0},{8,12},{12,8},{16,20},{20,16},{24,28},{28,24},{32,36},... | collective-permute-start | bytes 393224 | tf_op jit(solution)/shard_map/ppermute | solution.py:19
  97.7 3.2 %collective-permute-start.12 = (f32[1,32768]{1,0:T(1,128)S(1)}, f32[1,32768]{1,0:T(1,128)S(1)}, u32[]{:S(2)}, u32[]{:S(2)}) collective-permute-start(f32[1,32768]{1,0:T(1,128)S(1)} %get-tuple-element.11), channel_id=1, source_target_pairs={{0,4},{4,0},{8,12},{12,8},{16,20},{20,16},{24,28},{28,24},{32,36},... | collective-permute-start | bytes 393224 | tf_op jit(solution)/shard_map/ppermute | solution.py:19
  153.2 24.9 %copy-start = (f32[64,1,128]{2,1,0:T(1,128)S(1)}, f32[64,1,128]{2,1,0:T(1,128)}, u32[]{:S(2)}) copy-start(f32[64,1,128]{2,1,0:T(1,128)} %param.10) | copy-start | bytes 98308
  154.0 17.7 %all-to-all-start.1 = ((f32[128,1,64]{2,1,0:T(1,128)}), f32[128,1,64]{2,1,0:T(1,128)S(1)}, u32[]{:S(2)}, u32[]{:S(2)}) async-start(f32[128,1,64]{2,1,0:T(1,128)} %copy.119), calls=%async_computation.1 | async-start | bytes 131072 | tf_op jit(solution)/shard_map/all_to_all | solution.py:83
  171.7 21.1 %all-to-all-start = ((f32[128,1,512]{2,1,0:T(1,128)}), f32[128,1,512]{2,1,0:T(1,128)S(1)}, u32[]{:S(2)}, u32[]{:S(2)}) async-start(f32[128,1,512]{2,1,0:T(1,128)} %reshape.711), calls=%async_computation | async-start | bytes 524288 | tf_op jit(solution)/shard_map/all_to_all | solution.py:82
where the time goes:
time: 203 us; the launch traced here: 202 us
  starting transfers between devices  63.4 us (31%)
  waiting for transfers between devices  51.9 us (26%)
  local copies, waits for them, and re-layouts  46.5 us (23%)
  other arithmetic  15.7 us (8%)
  matrix products  14 us (7%)
  blocking collectives  9.04 us (4%)
    ppermute x13, starting transfers between devices, swapped(): lax.ppermute(shard, axis, [(i, i ^ 1 << apart) for i in range(lax.axis_si...  51.4 us
    ppermute x13, waiting for transfers between devices, swapped(): lax.ppermute(shard, axis, [(i, i ^ 1 << apart) for i in range(lax.axis_si...  38.3 us
    gather x2, local copies, waits for them, and re-layouts, strided_owners(): buffer = jnp.where(filled[:, :, None], payload[chosen], 0.0)  31.4 us
    all_to_all x1, waiting for transfers between devices, owner_relay(): lax.all_to_all(powers, 'bins', split_axis=0, concat_axis=0, tiled=True)  10.1 us
    psum x1, blocking collectives, body(): summed_power = lax.psum(partial_power, 'scans')  9.04 us
    sub x1, other arithmetic, rotate(): imag_part * cosine_part - real_part * sine_part  6.46 us
    all_to_all x1, starting transfers between devices, owner_relay(): lax.all_to_all(powers, 'bins', split_axis=0, concat_axis=0, tiled=True)  6.26 us
    all_to_all x1, starting transfers between devices, owner_relay(): lax.all_to_all(values, 'bins', split_axis=0, concat_axis=0, tiled=True)  5.75 us
  transfers between devices with their start and end apart: 15, of which 13 were waited for; matrix products, arithmetic and copies ran while one was open for 5% of the time, Pallas kernels for 0%

commit v1 on v0

v1 whole, which is shorter than its diff:
```python
import functools

import jax
import jax.numpy as jnp
import ml_dtypes
import numpy as np
from jax import lax
from jax.experimental import pallas as pl
from jax.experimental.pallas import tpu as pltpu
from jax.sharding import PartitionSpec as P

MESH = pl.DeviceIdType.MESH
BF=jnp.bfloat16; F32=jnp.float32
ND=128; NB=1<<22; M=1<<15; EPS=1e-5; NCLASS=5

def pair(a):
    a=np.asarray(a,np.float64)
    hi=a.astype(np.float32).astype(ml_dtypes.bfloat16)
    lo=(a-hi.astype(np.float64)).astype(np.float32).astype(ml_dtypes.bfloat16)
    return hi,lo
def split(x):
    hi=x.astype(BF); lo=(x-hi.astype(F32)).astype(BF)
    return hi,lo
def dot(a,b): return lax.dot_general(a,b,(((1,),(0,)),((),())),preferred_element_type=F32)
def dot_nt(a,b): return lax.dot_general(a,b,(((1,),(1,)),((),())),preferred_element_type=F32)
def dot3(a,b,d=dot):
    return d(a[0],b[0])+(d(a[0],b[1])+d(a[1],b[0]))
def tables():
    i=np.arange(128)[:,None]; j=np.arange(128)[None,:]; a=np.arange(256)[None,:]
    ang=2*np.pi*(i*j%128)/128; C,S=np.cos(ang),np.sin(ang)
    F1=np.concatenate([C,-S],0)
    MM=np.block([[C,S],[-S,C]])
    ang=2*np.pi*(i*a%256)/256; C2,S2=np.cos(ang),np.sin(ang)
    W2=np.block([[C2,S2],[-S2,C2]])
    ang=2*np.pi*(i*a)/M
    tw=np.stack([np.cos(ang),-np.sin(ang)]).astype(np.float32)
    b=np.arange(128)
    G=np.zeros((128,128))
    G[b,b//8]=1
    for m in range(16):
        g=15-m
        for bb in range(8*g+1,min(8*g+9,128)): G[bb,16+m]=1
    place=np.zeros((5,128,256))
    for q in range(5):
        for m in range(16):
            if q<4:
                place[q,m,16*q+m]=1; place[q,64+m,64+16*q+m]=1
                place[q,16+m,48-16*q+m]=1; place[q,80+m,64+48-16*q+m]=-1
        if q<4:
            place[q,40,128]=1; place[q,41,128]=1
        if q>=1:
            place[q,42,128]=1; place[q,32,64-16*q]=1; place[q,96,128-16*q]=-1
    place=place.reshape(640,256)
    co=np.zeros((5,128,128))
    for be in range(5):
        for k in range(64):
            co[be,k,k>>be]=1; co[be,64+k,64+(k>>be)]=1
    co=co.reshape(640,128)
    return dict(F1=pair(F1),MM=pair(MM),W2=pair(W2),tw=tw,G=G.astype(ml_dtypes.bfloat16),place=place.astype(ml_dtypes.bfloat16),co=co.astype(ml_dtypes.bfloat16))

def iota(shape,d): return lax.broadcasted_iota(jnp.int32,shape,d)

def stage1(R1, F1, W2, tw):
    A=dot3(F1, split(R1))
    Ar,Ai=A[:128],A[128:]
    tr,ti=tw[0],tw[1]
    Br=Ar*tr-Ai*ti; Bi=Ar*ti+Ai*tr
    B=jnp.concatenate([Br,Bi],1)
    Y=dot3(W2, split(B), dot_nt)
    Yr,Yi=Y[:128],Y[128:]
    lane=iota((1,256),1)
    nyq=jnp.sum(jnp.where(lane%2==0,Br[0:1],-Br[0:1]),axis=1,keepdims=True)
    first=(iota((128,128),0)==0)&(iota((128,128),1)==0)
    Yi=jnp.where(first,nyq,Yi)
    return jnp.concatenate([Yr,Yi],1)

def twiddle(me):
    n=iota((128,128),0); b=iota((128,128),1)
    th=(n*(128*me+b)).astype(F32)*(2*np.pi/NB)
    nn=n.astype(F32)*(2*np.pi/256)
    zero=me==0
    return jnp.cos(th),jnp.sin(th),jnp.cos(nn),jnp.sin(nn)

def stage2(R2, me, T, MM, G):
    Tr,Ts,Nr,Ns=T
    Rr,Ri=R2[:,:128],R2[:,128:]
    lane0=iota((128,128),1)==0
    zero=me==0
    Ri0=jnp.where(lane0&zero,0.0,Ri)
    Yr=Rr*Tr+Ri0*Ts; Yi=Ri0*Tr-Rr*Ts
    Er=jnp.where(zero,Ri*Nr,Yr); Ei=jnp.where(zero,-Ri*Ns,Yi)
    Y=jnp.concatenate([Yr,Yi],0); E=jnp.concatenate([Er,Ei],0)
    yh,yl=split(Y)
    Z=dot(yh,G)+dot(yl,G)
    Z=jnp.where(iota((256,128),1)==32,E[:,0:1],Z)
    zh,zl=split(Z)
    X=dot3(MM,(jnp.concatenate([yh,zh],1),jnp.concatenate([yl,zl],1)))
    Xr,Xi=X[:128,:128],X[128:,:128]; Fr,Fi=X[:128,128:],X[128:,128:]
    rows=iota((128,128),0)
    Pw=Xr*Xr+Xi*Xi
    Pw=jnp.where(lane0&(rows>=64),0.0,Pw)
    ps=jnp.sum(Pw,axis=1,keepdims=True)
    Pe=(Fr*Fr+Fi*Fi)
    lane=iota((128,128),1)
    Q=jnp.where(lane==0,ps,jnp.where(lane==32,Pe,0.0))
    Qt=jnp.transpose(Q)
    return Fr,Fi,Qt

def starts_of(counts_row):
    o=iota((128,128),0); k=iota((128,128),1)
    return jnp.sum(jnp.where(k<o,counts_row.astype(F32),0.0),axis=1,keepdims=True).astype(jnp.int32)

def onehots(starts, me):
    q4=me//4
    k=iota((128,128),1)
    def row(cl):
        return (starts+((cl-starts)&63))>>6
    main=row(q4); mir=127-row(63-q4); ext=127-row(63-((me+127)%128)//4)
    Sm=(k==main)&(k<64); Sx=(k==mir)&(k>=64); Se=(k==ext)&(k>=64)
    return Sm,Sx,Se

def stage3(Fr,Fi,S):
    Sm,Sx,Se=S
    rows=iota((128,128),0); lane=iota((128,128),1)
    keep=((rows<64)&(lane<16))|((rows>=64)&(lane>=16)&(lane<32))
    keepe=(rows>=64)&(lane==32)
    Wm=jnp.concatenate([jnp.where(keep,Fr,0.0),jnp.where(keep,Fi,0.0)],1)
    We=jnp.concatenate([jnp.where(keepe,Fr,0.0),jnp.where(keepe,Fi,0.0)],1)
    W=jnp.concatenate([Wm,We],0)
    SS=jnp.concatenate([(Sm|Sx).astype(F32).astype(BF),Se.astype(F32).astype(BF)],1)
    h,l=split(W)
    Ms=dot(SS,h)+dot(SS,l)
    return Ms[:,:128], Ms[:,128:]

def stage3b(mr,mi_rolled,S,tot):
    Sm,Sx,Se=S
    p0=tot[0:1]; p1=tot[1:2]
    z=0.0
    a=jnp.sum(jnp.where(Sm,p0,z),axis=1,keepdims=True)
    b=jnp.sum(jnp.where(Sx,p0,z),axis=1,keepdims=True)
    c=jnp.sum(jnp.where(Se,p1,z),axis=1,keepdims=True)
    lane=iota((128,128),1)
    return jnp.where(lane<40,mr,jnp.where(lane>=64,mi_rolled,jnp.where(lane==40,a,jnp.where(lane==41,b,jnp.where(lane==42,c,0.0)))))

def slot_info(counts_row, edges, me):
    k=iota((64,128),1)
    st=jnp.sum(jnp.where(k<me,counts_row.astype(F32),0.0),axis=1,keepdims=True).astype(jnp.int32)
    cn=jnp.sum(jnp.where(k==me,counts_row.astype(F32),0.0),axis=1,keepdims=True).astype(jnp.int32)
    s=iota((64,1),0)
    t=st+s
    band=sum([(t>=edges[e]).astype(jnp.int32) for e in range(1,5)])
    return t,band,s<cn

def owner_select(t):
    c=t&63; main=c<32
    j=iota((64,128),1)
    r4=4*jnp.where(main,c,63-c)
    sel=[(j==r4+q).astype(F32).astype(BF) for q in range(4)]
    sel.append((j==((4*(64-c))&127)).astype(F32).astype(BF))
    return jnp.concatenate(sel,0)

def state_part(prev, dyn, t, band):
    pr=jnp.concatenate([prev[:,:64],prev[:,64:]],0)
    band2=jnp.concatenate([band,band],0)
    cnt=64>>band2
    lane=iota((128,64),1)
    pr=jnp.where(lane<cnt,pr,0.0)
    out=jnp.zeros((128,64),F32)
    for be in range(NCLASS):
        x=jnp.where(band2==be,pr,0.0)
        out=out+dot3(split(x),split(dyn[be]),dot_nt)
    out=jnp.where(lane<cnt,out,0.0)
    return jnp.concatenate([out[:64],out[64:]],1)

def stage4(R3, sel, t, band, occ, place, co, spart):
    h,l=split(R3)
    main=(t&63)<32
    lane=iota((64,128),1)
    inmain=(lane<16)|((lane>=64)&(lane<80))|(lane==40)
    inmir=((lane>=16)&(lane<32))|((lane>=80)&(lane<96))|(lane==41)
    inext=(lane==32)|(lane==96)|(lane==42)
    res=None
    for v in (h,l):
        T=dot(sel,v)
        parts=[]
        for q in range(5):
            mk=(main&inmain&(q<4))|(jnp.logical_not(main)&((inmir&(q<4))|(inext&(q>=1))))
            parts.append(jnp.where(mk,T[64*q:64*q+64],0.0).astype(BF))
        o=dot(jnp.concatenate(parts,1),place)
        res=o if res is None else res+o
    fine=res[:,:128]; pw=res[:,128:129]
    fh,fl=split(fine)
    meas=None
    for v in (fh,fl):
        x=jnp.concatenate([jnp.where(band==be,v.astype(F32),0.0).astype(BF) for be in range(5)],1)
        o=dot(x,co)
        meas=o if meas is None else meas+o
    mp=pw/(4*512)
    scale=1.0/jnp.sqrt((8<<band).astype(F32)*(mp+EPS))
    st=iota((64,128),1)&63
    meas=jnp.where(st<(64>>band),meas*scale,0.0)
    return jnp.where(occ,meas+spart,0.0)


def kernel(edges_ref, x_h, cnt_h, dyn_h, prev_h, f1h_h, f1l_h, mmh_h, mml_h, w2h_h, w2l_h, tw_h, g_h, pl_h, co_h,
           o_ref,
           x_v, cnt_v, dyn_v, prev_v, f1h_v, f1l_v, mmh_v, mml_v, w2h_v, w2l_v, tw_v, g_v, pl_v, co_v,
           s1, r1, s2, r2, s3, r3, xs, xr, dummy, t_v, oh_v, sp_v, sel_v, csem, sem):
    me = lax.axis_index("bins")
    mx = lax.axis_index("scans")
    hs = [x_h, cnt_h, dyn_h, prev_h, f1h_h, f1l_h, mmh_h, mml_h, w2h_h, w2l_h, tw_h, g_h, pl_h, co_h]
    vs = [x_v, cnt_v, dyn_v, prev_v, f1h_v, f1l_v, mmh_v, mml_v, w2h_v, w2l_v, tw_v, g_v, pl_v, co_v]
    loads = [pltpu.make_async_copy(h, v, csem.at[i]) for i, (h, v) in enumerate(zip(hs, vs))]
    loads[0].start()
    bar = pltpu.get_barrier_semaphore()

    def sig(i, c):
        pl.semaphore_signal(bar, inc=1, device_id={"bins": lax.rem(me + i, ND)}, device_id_type=MESH)
        return c

    lax.fori_loop(1, ND, sig, 0)
    for i in range(1, 4):
        pl.semaphore_signal(bar, inc=1, device_id={"scans": lax.rem(mx + i, 4)}, device_id_type=MESH)
    for ld in loads[1:]:
        ld.start()
    loads[0].wait()
    s1[...] = jnp.concatenate([jnp.transpose(x_v[0:128, :]), jnp.transpose(x_v[128:256, :])], 1)
    pl.semaphore_wait(bar, ND + 2)

    def send_all(s, r, k):
        def one(i, c):
            j = lax.rem(me + i, ND)
            pltpu.make_async_remote_copy(s.at[pl.ds(j, 1)], r.at[pl.ds(me, 1)], sem.at[k], sem.at[k + 1],
                                         device_id={"bins": j}, device_id_type=MESH).start()
            return c
        lax.fori_loop(1, ND, one, 0)

    def wait_all(w, k):
        d = dummy.at[:, :, pl.ds(0, w)]
        pltpu.make_async_copy(d, d, sem.at[k]).wait()

    send_all(s1, r1, 0)
    r1[pl.ds(me, 1), :] = s1[pl.ds(me, 1), :]
    for ld in loads[1:]:
        ld.wait()
    T = twiddle(me)
    for i in range(4):
        t_v[i] = T[i]
    counts = cnt_v[...]
    for i, m in enumerate(onehots(starts_of(counts), me)):
        oh_v[i] = m.astype(F32)
    edges = [edges_ref[i] for i in range(6)]
    t, band, occ = slot_info(counts, edges, me)
    sp_v[...] = state_part(prev_v[...], dyn_v, t, band)
    sel_v[...] = owner_select(t)
    wait_all(256, 1)
    wait_all(256, 0)

    s2[...] = stage1(r1[...], (f1h_v[...], f1l_v[...]), (w2h_v[...], w2l_v[...]), tw_v)
    send_all(s2, r2, 2)
    r2[pl.ds(me, 1), :] = s2[pl.ds(me, 1), :]
    wait_all(256, 3)
    wait_all(256, 2)

    Fr, Fi, Qt = stage2(r2[...], me, [t_v[i] for i in range(4)], (mmh_v[...], mml_v[...]), g_v[...])
    xs[...] = Qt[0:8]
    xs[1:2, :] = Qt[32:33]
    for i in range(1, 4):
        pltpu.make_async_remote_copy(xs, xr.at[mx], sem.at[4], sem.at[5],
                                     device_id={"scans": lax.rem(mx + i, 4)}, device_id_type=MESH).start()
    xr[mx] = xs[...]
    S = [oh_v[i] > 0.5 for i in range(3)]
    mr, mi = stage3(Fr, Fi, S)
    mi = pltpu.roll(mi, 64, 1)
    d = xr.at[pl.ds(0, 3)]
    pltpu.make_async_copy(d, d, sem.at[5]).wait()
    pltpu.make_async_copy(d, d, sem.at[4]).wait()
    tot = xr[0] + xr[1] + xr[2] + xr[3]
    s3[...] = stage3b(mr, mi, S, tot)
    send_all(s3, r3, 6)
    r3[pl.ds(me, 1), :] = s3[pl.ds(me, 1), :]
    wait_all(128, 7)
    wait_all(128, 6)
    t, band, occ = slot_info(cnt_v[...], edges, me)
    o_ref[...] = stage4(r3[...], sel_v[...], t, band, occ, pl_v[...], co_v[...], sp_v[...])


def body(profiles, band_edges, owner_counts, dynamics, prev_state):
    tb = tables()
    consts = [*tb["F1"], *tb["MM"], *tb["W2"], tb["tw"], tb["G"], tb["place"], tb["co"]]
    ins = [profiles.reshape(256, 128), owner_counts.reshape(1, 128), dynamics, prev_state.reshape(64, 128)]
    ins += [jnp.asarray(c) for c in consts]
    V = pltpu.VMEM
    out = pl.pallas_call(
        kernel,
        out_shape=jax.ShapeDtypeStruct((64, 128), F32),
        in_specs=[pl.BlockSpec(memory_space=pltpu.SMEM)] + [pl.BlockSpec(memory_space=pl.ANY)] * len(ins),
        out_specs=pl.BlockSpec(memory_space=V),
        scratch_shapes=[V(i.shape, i.dtype) for i in ins] + [
            V((128, 256), F32), V((128, 256), F32), V((128, 256), F32), V((128, 256), F32),
            V((128, 128), F32), V((128, 128), F32), V((8, 128), F32), V((4, 8, 128), F32),
            V((127, 1, 256), F32), V((4, 128, 128), F32), V((3, 128, 128), F32), V((64, 128), F32), V((320, 128), BF),
            pltpu.SemaphoreType.DMA((len(ins),)), pltpu.SemaphoreType.DMA((8,))],
        compiler_params=pltpu.CompilerParams(collective_id=0, has_side_effects=True),
    )(band_edges, *ins)
    return out.reshape(64, 1, 128)


def solution(mesh):
    return jax.shard_map(
        body,
        mesh=mesh,
        in_specs=(P("scans", "bins"), P(), P(), P(), P("bins", "scans", None)),
        out_specs=P("bins", "scans", None),
        check_vma=False,
    )
```

time: 203 us -> 50.7 us (0.25)
  starting transfers between devices: 63.4 us -> 0 us
  waiting for transfers between devices: 51.9 us -> 0 us
  Pallas kernels: 0 us -> 49.1 us
  local copies, waits for them, and re-layouts: 46.5 us -> 1.38 us
  other arithmetic: 15.7 us -> 0 us
  matrix products: 14 us -> 0 us
  blocking collectives: 9.04 us -> 0 us
    ppermute x13 -> x0, starting transfers between devices: 51.4 us -> none  [swapped(): lax.ppermute(shard, axis, [(i, i ^ 1 << apart) for i in range(lax.axis_si...]
    pallas_call x0 -> x1, Pallas kernels: none -> 49.1 us  [body(): pl.pallas_call(kernel, out_shape=jax.ShapeDtypeStruct((64, 128), F32), in...]
    ppermute x13 -> x0, waiting for transfers between devices: 38.3 us -> none  [swapped(): lax.ppermute(shard, axis, [(i, i ^ 1 << apart) for i in range(lax.axis_si...]
    gather x2 -> x0, local copies, waits for them, and re-layouts: 31.4 us -> none  [strided_owners(): buffer = jnp.where(filled[:, :, None], payload[chosen], 0.0)]
    dot_general x11 -> x0, matrix products: 14 us -> none  [the longest x1 5.22 us: update(): jnp.einsum('rij,rpcj->rpci', picked, previous, precision=HIGHEST) + measured]
    all_to_all x2 -> x0, waiting for transfers between devices: 13.6 us -> none  [the longest x1 10.1 us: owner_relay(): lax.all_to_all(powers, 'bins', split_axis=0, concat_axis=0, tiled=True)]
    all_to_all x2 -> x0, starting transfers between devices: 12 us -> none  [the longest x1 6.26 us: owner_relay(): lax.all_to_all(powers, 'bins', split_axis=0, concat_axis=0, tiled=True)]
    psum x1 -> x0, blocking collectives: 9.04 us -> none  [body(): summed_power = lax.psum(partial_power, 'scans')]
  transfers between devices with their start and end apart: 15 -> 0, of which waited for: 13 -> 0; matrix products, arithmetic and copies ran while one was open for 5% -> 0% of each run, Pallas kernels for 0% -> 0%
where the time goes in v1:
time: 50.7 us; the launch traced here: 50.5 us
  Pallas kernels  49.1 us (97%)
  local copies, waits for them, and re-layouts  1.38 us (3%)
    pallas_call x1, Pallas kernels, body(): pl.pallas_call(kernel, out_shape=jax.ShapeDtypeStruct((64, 128), F32), in...  49.1 us
    unnamed x1, local copies, waits for them, and re-layouts  1.38 us

profile of v1, /device:TPU:1, one launch (start us, length us, event | category | flops | bytes accessed | tf_op | source)
XLA Modules:
  0.0 50.5 jit_solution(157211854567448775)
XLA Ops:
  0.0 49.1 %shard_map.145 = f32[64,128]{1,0:T(8,128)} custom-call(s32[6]{0:T(128)} %edges_ref.1, f32[256,128]{1,0:T(8,128)} %bitcast.7, s32[1,128]{1,0:T(1,128)} %bitcast.9, f32[5,64,64]{2,1,0:T(8,128)} %dyn_h.1, f32[64,128]{1,0:T(8,128)} %bitcast.8, bf16[256,128]{1,0:T(8,128)(2,1)} %constant.20.clone.f1h_h, bf16[256,128]{1,0:T(8,128)(2,1)} %constant.21.clone.f1l_h, ...), custom_call_target="tpu_custom_call" | custom-call | tf_op jit(solution)/shard_map/pallas_call | solution.py:294
  49.1 1.4 %copy.18 = f32[64,1,128]{2,1,0:T(1,128)} copy(f32[64,1,128]{2,1,0:T(1,128)} %bitcast.6) | data formatting | bytes 65536

commit v2 on v1

--- a/solution.py
+++ b/solution.py
@@ -214,11 +214,21 @@
     loads[0].start()
     bar = pltpu.get_barrier_semaphore()
 
-    def sig(i, c):
-        pl.semaphore_signal(bar, inc=1, device_id={"bins": lax.rem(me + i, ND)}, device_id_type=MESH)
-        return c
-
-    lax.fori_loop(1, ND, sig, 0)
+    z16, y2, c1 = me & 112, me & 14, me & 1
+    ys = [((y2 + 2 * d) & 14) | (c1 ^ c) for d in (4, 3, 5, 2, 6, 1, 7, 0) for c in (1, 0)]
+
+    def far_first(act):
+        def ring(i, c):
+            d = 4 + jnp.where((i & 1) == 1, -((i + 1) >> 1), i >> 1)
+            zz = (z16 + 16 * d) & 112
+            for y in ys:
+                act(zz | y)
+            return c
+        lax.fori_loop(0, 7, ring, 0)
+        for y in ys[:-1]:
+            act(z16 | y)
+
+    far_first(lambda j: pl.semaphore_signal(bar, inc=1, device_id={"bins": j}, device_id_type=MESH))
     for i in range(1, 4):
         pl.semaphore_signal(bar, inc=1, device_id={"scans": lax.rem(mx + i, 4)}, device_id_type=MESH)
     for ld in loads[1:]:
@@ -228,12 +238,10 @@
     pl.semaphore_wait(bar, ND + 2)
 
     def send_all(s, r, k):
-        def one(i, c):
-            j = lax.rem(me + i, ND)
+        def one(j):
             pltpu.make_async_remote_copy(s.at[pl.ds(j, 1)], r.at[pl.ds(me, 1)], sem.at[k], sem.at[k + 1],
                                          device_id={"bins": j}, device_id_type=MESH).start()
-            return c
-        lax.fori_loop(1, ND, one, 0)
+        far_first(one)
 
     def wait_all(w, k):
         d = dummy.at[:, :, pl.ds(0, w)]
@@ -297,8 +305,7 @@
         in_specs=[pl.BlockSpec(memory_space=pltpu.SMEM)] + [pl.BlockSpec(memory_space=pl.ANY)] * len(ins),
         out_specs=pl.BlockSpec(memory_space=V),
         scratch_shapes=[V(i.shape, i.dtype) for i in ins] + [
-            V((128, 256), F32), V((128, 256), F32), V((128, 256), F32), V((128, 256), F32),
-            V((128, 128), F32), V((128, 128), F32), V((8, 128), F32), V((4, 8, 128), F32),
+            *[V((128, 256), F32)] * 4, *[V((128, 128), F32)] * 2, V((8, 128), F32), V((4, 8, 128), F32),
             V((127, 1, 256), F32), V((4, 128, 128), F32), V((3, 128, 128), F32), V((64, 128), F32), V((320, 128), BF),
             pltpu.SemaphoreType.DMA((len(ins),)), pltpu.SemaphoreType.DMA((8,))],
         compiler_params=pltpu.CompilerParams(collective_id=0, has_side_effects=True),

time: 50.7 us -> 46.8 us (0.923)
  Pallas kernels: 49.1 us -> 45.3 us
    pallas_call x1, Pallas kernels: 49.1 us -> 45.3 us  [body(): pl.pallas_call(kernel, out_shape=jax.ShapeDtypeStruct((64, 128), F32), in...]
where the time goes in v2:
time: 46.8 us; the launch traced here: 46.6 us
  Pallas kernels  45.3 us (97%)
  local copies, waits for them, and re-layouts  1.38 us (3%)
    pallas_call x1, Pallas kernels, body(): pl.pallas_call(kernel, out_shape=jax.ShapeDtypeStruct((64, 128), F32), in...  45.3 us
    unnamed x1, local copies, waits for them, and re-layouts  1.38 us

profile of v2, /device:TPU:1, one launch (start us, length us, event | category | flops | bytes accessed | tf_op | source)
XLA Modules:
  0.0 46.6 jit_solution(688544535618747005)
XLA Ops:
  0.0 45.3 %shard_map.145 = f32[64,128]{1,0:T(8,128)} custom-call(s32[6]{0:T(128)} %edges_ref.1, f32[256,128]{1,0:T(8,128)} %bitcast.7, s32[1,128]{1,0:T(1,128)} %bitcast.9, f32[5,64,64]{2,1,0:T(8,128)} %dyn_h.1, f32[64,128]{1,0:T(8,128)} %bitcast.8, bf16[256,128]{1,0:T(8,128)(2,1)} %constant.20.clone.f1h_h, bf16[256,128]{1,0:T(8,128)(2,1)} %constant.21.clone.f1l_h, ...), custom_call_target="tpu_custom_call" | custom-call | tf_op jit(solution)/shard_map/pallas_call | solution.py:302
  45.3 1.4 %copy.18 = f32[64,1,128]{2,1,0:T(1,128)} copy(f32[64,1,128]{2,1,0:T(1,128)} %bitcast.6) | data formatting | bytes 65536

commit v3 on v2

--- a/solution.py
+++ b/solution.py
@@ -202,14 +202,14 @@
     return jnp.where(occ,meas+spart,0.0)
 
 
-def kernel(edges_ref, x_h, cnt_h, dyn_h, prev_h, f1h_h, f1l_h, mmh_h, mml_h, w2h_h, w2l_h, tw_h, g_h, pl_h, co_h,
+def kernel(x_h, cnt_h, edges_h, dyn_h, prev_h, f1h_h, f1l_h, mmh_h, mml_h, w2h_h, w2l_h, tw_h, g_h, pl_h, co_h,
            o_ref,
-           x_v, cnt_v, dyn_v, prev_v, f1h_v, f1l_v, mmh_v, mml_v, w2h_v, w2l_v, tw_v, g_v, pl_v, co_v,
+           x_v, cnt_v, edges_v, dyn_v, prev_v, f1h_v, f1l_v, mmh_v, mml_v, w2h_v, w2l_v, tw_v, g_v, pl_v, co_v,
            s1, r1, s2, r2, s3, r3, xs, xr, dummy, t_v, oh_v, sp_v, sel_v, csem, sem):
     me = lax.axis_index("bins")
     mx = lax.axis_index("scans")
-    hs = [x_h, cnt_h, dyn_h, prev_h, f1h_h, f1l_h, mmh_h, mml_h, w2h_h, w2l_h, tw_h, g_h, pl_h, co_h]
-    vs = [x_v, cnt_v, dyn_v, prev_v, f1h_v, f1l_v, mmh_v, mml_v, w2h_v, w2l_v, tw_v, g_v, pl_v, co_v]
+    hs = [x_h, cnt_h, edges_h, dyn_h, prev_h, f1h_h, f1l_h, mmh_h, mml_h, w2h_h, w2l_h, tw_h, g_h, pl_h, co_h]
+    vs = [x_v, cnt_v, edges_v, dyn_v, prev_v, f1h_v, f1l_v, mmh_v, mml_v, w2h_v, w2l_v, tw_v, g_v, pl_v, co_v]
     loads = [pltpu.make_async_copy(h, v, csem.at[i]) for i, (h, v) in enumerate(zip(hs, vs))]
     loads[0].start()
     bar = pltpu.get_barrier_semaphore()
@@ -257,7 +257,7 @@
     counts = cnt_v[...]
     for i, m in enumerate(onehots(starts_of(counts), me)):
         oh_v[i] = m.astype(F32)
-    edges = [edges_ref[i] for i in range(6)]
+    edges = [edges_v[i] for i in range(6)]
     t, band, occ = slot_info(counts, edges, me)
     sp_v[...] = state_part(prev_v[...], dyn_v, t, band)
     sel_v[...] = owner_select(t)
@@ -293,23 +293,29 @@
     o_ref[...] = stage4(r3[...], sel_v[...], t, band, occ, pl_v[...], co_v[...], sp_v[...])
 
 
+def emit(a_ref, o_ref, sem):
+    c = pltpu.make_async_copy(a_ref, o_ref, sem)
+    c.start()
+    c.wait()
+
+
 def body(profiles, band_edges, owner_counts, dynamics, prev_state):
     tb = tables()
     consts = [*tb["F1"], *tb["MM"], *tb["W2"], tb["tw"], tb["G"], tb["place"], tb["co"]]
-    ins = [profiles.reshape(256, 128), owner_counts.reshape(1, 128), dynamics, prev_state.reshape(64, 128)]
+    ins = [profiles.reshape(256, 128), owner_counts.reshape(1, 128), band_edges, dynamics, prev_state.reshape(64, 128)]
     ins += [jnp.asarray(c) for c in consts]
     V = pltpu.VMEM
     out = pl.pallas_call(
         kernel,
-        out_shape=jax.ShapeDtypeStruct((64, 128), F32),
-        in_specs=[pl.BlockSpec(memory_space=pltpu.SMEM)] + [pl.BlockSpec(memory_space=pl.ANY)] * len(ins),
+        out_shape=V((64, 128), F32),
+        in_specs=[pl.BlockSpec(memory_space=pltpu.HBM)] * len(ins),
         out_specs=pl.BlockSpec(memory_space=V),
-        scratch_shapes=[V(i.shape, i.dtype) for i in ins] + [
+        scratch_shapes=[(pltpu.SMEM if i.shape == (6,) else V)(i.shape, i.dtype) for i in ins] + [
             *[V((128, 256), F32)] * 4, *[V((128, 128), F32)] * 2, V((8, 128), F32), V((4, 8, 128), F32),
             V((127, 1, 256), F32), V((4, 128, 128), F32), V((3, 128, 128), F32), V((64, 128), F32), V((320, 128), BF),
             pltpu.SemaphoreType.DMA((len(ins),)), pltpu.SemaphoreType.DMA((8,))],
-        compiler_params=pltpu.CompilerParams(collective_id=0, has_side_effects=True),
-    )(band_edges, *ins)
+        compiler_params=pltpu.CompilerParams(collective_id=0, has_side_effects=True, vmem_limit_bytes=48 << 20),
+    )(*[pltpu.with_memory_space_constraint(i, pltpu.HBM) for i in ins])
     return out.reshape(64, 1, 128)
 
 

time: 46.8 us -> 44.7 us (0.955)
  Pallas kernels: 45.3 us -> 44 us
  local copies, waits for them, and re-layouts: 1.38 us -> 0.62 us
    pallas_call x1, Pallas kernels: 45.3 us -> 44 us  [body(): pl.pallas_call(kernel, out_shape=V((64, 128), F32), in_specs=[pl.BlockSpe...]
    unnamed x1, local copies, waits for them, and re-layouts: 1.38 us -> 0.62 us
where the time goes in v3:
time: 44.7 us; the launch traced here: 44.6 us
  Pallas kernels  44 us (98%)
  local copies, waits for them, and re-layouts  0.62 us (1%)
    pallas_call x1, Pallas kernels, body(): pl.pallas_call(kernel, out_shape=V((64, 128), F32), in_specs=[pl.BlockSpe...  44 us

profile of v3, /device:TPU:1, one launch (start us, length us, event | category | flops | bytes accessed | tf_op | source)
XLA Modules:
  0.0 44.6 jit_solution(17765043220657939833)
XLA Ops:
  0.0 44.0 %shard_map.145 = f32[64,128]{1,0:T(8,128)S(1)} custom-call(f32[256,128]{1,0:T(8,128)} %bitcast.7, s32[1,128]{1,0:T(1,128)} %bitcast.9, s32[6]{0:T(128)} %edges_h.1, f32[5,64,64]{2,1,0:T(8,128)} %dyn_h.1, f32[64,128]{1,0:T(8,128)} %bitcast.8, bf16[256,128]{1,0:T(8,128)(2,1)} %constant.20.clone.f1h_h, bf16[256,128]{1,0:T(8,128)(2,1)} %constant.21.clone.f1l_h, ...), custom_call_target="tpu_custom_call" | custom-call | tf_op jit(solution)/shard_map/pallas_call | solution.py:308
  44.0 0.6 %copy.18 = f32[64,1,128]{2,1,0:T(1,128)} copy(f32[64,1,128]{2,1,0:T(1,128)S(1)} %bitcast.6) | data formatting | bytes 65536

commit v4 on v3

--- a/solution.py
+++ b/solution.py
@@ -31,7 +31,7 @@
     F1=np.concatenate([C,-S],0)
     MM=np.block([[C,S],[-S,C]])
     ang=2*np.pi*(i*a%256)/256; C2,S2=np.cos(ang),np.sin(ang)
-    W2=np.block([[C2,S2],[-S2,C2]])
+    W2=np.block([[C2,S2]])
     ang=2*np.pi*(i*a)/M
     tw=np.stack([np.cos(ang),-np.sin(ang)]).astype(np.float32)
     b=np.arange(128)
@@ -56,23 +56,26 @@
         for k in range(64):
             co[be,k,k>>be]=1; co[be,64+k,64+(k>>be)]=1
     co=co.reshape(640,128)
-    return dict(F1=pair(F1),MM=pair(MM),W2=pair(W2),tw=tw,G=G.astype(ml_dtypes.bfloat16),place=place.astype(ml_dtypes.bfloat16),co=co.astype(ml_dtypes.bfloat16))
+    f1h,f1l=pair(F1)
+    return dict(F1=(np.concatenate([f1h,f1h],1),f1l),MM=pair(MM),W2=pair(W2),tw=tw,G=np.concatenate([G,G],0).astype(ml_dtypes.bfloat16),place=place.astype(ml_dtypes.bfloat16),co=co.astype(ml_dtypes.bfloat16))
 
 def iota(shape,d): return lax.broadcasted_iota(jnp.int32,shape,d)
 
 def stage1(R1, F1, W2, tw):
-    A=dot3(F1, split(R1))
+    gh,gl=split(R1)
+    A=dot(F1[0],jnp.concatenate([gh,gl],0))+dot(F1[1],gh)
     Ar,Ai=A[:128],A[128:]
     tr,ti=tw[0],tw[1]
     Br=Ar*tr-Ai*ti; Bi=Ar*ti+Ai*tr
-    B=jnp.concatenate([Br,Bi],1)
-    Y=dot3(W2, split(B), dot_nt)
-    Yr,Yi=Y[:128],Y[128:]
+    (rh,rl),(ih,il)=split(Br),split(Bi)
+    def both(r,i):
+        return jnp.concatenate([jnp.concatenate([r,i],1),jnp.concatenate([i,-r],1)],0)
+    Y=dot3(W2, (both(rh,ih),both(rl,il)), dot_nt)
     lane=iota((1,256),1)
     nyq=jnp.sum(jnp.where(lane%2==0,Br[0:1],-Br[0:1]),axis=1,keepdims=True)
-    first=(iota((128,128),0)==0)&(iota((128,128),1)==0)
-    Yi=jnp.where(first,nyq,Yi)
-    return jnp.concatenate([Yr,Yi],1)
+    first=(iota((128,256),0)==0)&(iota((128,256),1)==128)
+    Y=jnp.where(first,nyq,Y)
+    return Y[:,:128],Y[:,128:]
 
 def twiddle(me):
     n=iota((128,128),0); b=iota((128,128),1)
@@ -81,7 +84,7 @@
     zero=me==0
     return jnp.cos(th),jnp.sin(th),jnp.cos(nn),jnp.sin(nn)
 
-def stage2(R2, me, T, MM, G):
+def stage2(R2, me, T, MM):
     Tr,Ts,Nr,Ns=T
     Rr,Ri=R2[:,:128],R2[:,128:]
     lane0=iota((128,128),1)==0
@@ -90,21 +93,20 @@
     Yr=Rr*Tr+Ri0*Ts; Yi=Ri0*Tr-Rr*Ts
     Er=jnp.where(zero,Ri*Nr,Yr); Ei=jnp.where(zero,-Ri*Ns,Yi)
     Y=jnp.concatenate([Yr,Yi],0); E=jnp.concatenate([Er,Ei],0)
-    yh,yl=split(Y)
-    Z=dot(yh,G)+dot(yl,G)
-    Z=jnp.where(iota((256,128),1)==32,E[:,0:1],Z)
-    zh,zl=split(Z)
-    X=dot3(MM,(jnp.concatenate([yh,zh],1),jnp.concatenate([yl,zl],1)))
-    Xr,Xi=X[:128,:128],X[128:,:128]; Fr,Fi=X[:128,128:],X[128:,128:]
+    yh,yl=split(Y); eh,el=split(E)
+    X=dot3(MM,(jnp.concatenate([yh,eh],1),jnp.concatenate([yl,el],1)))
+    Xr,Xi,Er,Ei=X[:128,:128],X[128:,:128],X[:128,128:],X[128:,128:]
     rows=iota((128,128),0)
-    Pw=Xr*Xr+Xi*Xi
-    Pw=jnp.where(lane0&(rows>=64),0.0,Pw)
-    ps=jnp.sum(Pw,axis=1,keepdims=True)
-    Pe=(Fr*Fr+Fi*Fi)
-    lane=iota((128,128),1)
-    Q=jnp.where(lane==0,ps,jnp.where(lane==32,Pe,0.0))
-    Qt=jnp.transpose(Q)
-    return Fr,Fi,Qt
+    Pw=jnp.where(lane0&(rows>=64),0.0,Xr*Xr+Xi*Xi)
+    Pe=jnp.where(lane0,Er*Er+Ei*Ei,0.0)
+    ph,pl_=split(jnp.concatenate([Pw,Pe],0))
+    sums=dot_nt(jnp.ones((8,256),BF),jnp.concatenate([ph,pl_],1))
+    return sums,(yh,yl),(Er,Ei)
+
+def stage2b(y, E, MM, G):
+    Z=dot(jnp.concatenate(y,1),G)
+    F=dot3(MM,split(Z))
+    return F[:128],F[128:]
 
 def starts_of(counts_row):
     o=iota((128,128),0); k=iota((128,128),1)
@@ -119,13 +121,13 @@
     Sm=(k==main)&(k<64); Sx=(k==mir)&(k>=64); Se=(k==ext)&(k>=64)
     return Sm,Sx,Se
 
-def stage3(Fr,Fi,S):
+def stage3(Fr,Fi,E,S):
     Sm,Sx,Se=S
     rows=iota((128,128),0); lane=iota((128,128),1)
     keep=((rows<64)&(lane<16))|((rows>=64)&(lane>=16)&(lane<32))
     keepe=(rows>=64)&(lane==32)
     Wm=jnp.concatenate([jnp.where(keep,Fr,0.0),jnp.where(keep,Fi,0.0)],1)
-    We=jnp.concatenate([jnp.where(keepe,Fr,0.0),jnp.where(keepe,Fi,0.0)],1)
+    We=jnp.concatenate([jnp.where(keepe,E[0][:,0:1],0.0),jnp.where(keepe,E[1][:,0:1],0.0)],1)
     W=jnp.concatenate([Wm,We],0)
     SS=jnp.concatenate([(Sm|Sx).astype(F32).astype(BF),Se.astype(F32).astype(BF)],1)
     h,l=split(W)
@@ -134,7 +136,7 @@
 
 def stage3b(mr,mi_rolled,S,tot):
     Sm,Sx,Se=S
-    p0=tot[0:1]; p1=tot[1:2]
+    p0=tot[0:1]; p1=tot[4:5]
     z=0.0
     a=jnp.sum(jnp.where(Sm,p0,z),axis=1,keepdims=True)
     b=jnp.sum(jnp.where(Sx,p0,z),axis=1,keepdims=True)
@@ -179,27 +181,34 @@
     inmain=(lane<16)|((lane>=64)&(lane<80))|(lane==40)
     inmir=((lane>=16)&(lane<32))|((lane>=80)&(lane<96))|(lane==41)
     inext=(lane==32)|(lane==96)|(lane==42)
-    res=None
-    for v in (h,l):
-        T=dot(sel,v)
+    T=dot(sel,jnp.concatenate([h,l],1))
+    halves=[]
+    for v in (T[:,:128],T[:,128:]):
         parts=[]
         for q in range(5):
             mk=(main&inmain&(q<4))|(jnp.logical_not(main)&((inmir&(q<4))|(inext&(q>=1))))
-            parts.append(jnp.where(mk,T[64*q:64*q+64],0.0).astype(BF))
-        o=dot(jnp.concatenate(parts,1),place)
-        res=o if res is None else res+o
+            parts.append(jnp.where(mk,v[64*q:64*q+64],0.0).astype(BF))
+        halves.append(jnp.concatenate(parts,1))
+    res=dot(jnp.concatenate(halves,0),place)
+    res=res[:64]+res[64:]
     fine=res[:,:128]; pw=res[:,128:129]
-    fh,fl=split(fine)
-    meas=None
-    for v in (fh,fl):
-        x=jnp.concatenate([jnp.where(band==be,v.astype(F32),0.0).astype(BF) for be in range(5)],1)
-        o=dot(x,co)
-        meas=o if meas is None else meas+o
+    fhl=jnp.concatenate(split(fine),0).astype(F32)
+    band2=jnp.concatenate([band,band],0)
+    x=jnp.concatenate([jnp.where(band2==be,fhl,0.0).astype(BF) for be in range(5)],1)
+    meas=dot(x,co)
+    meas=meas[:64]+meas[64:]
     mp=pw/(4*512)
     scale=1.0/jnp.sqrt((8<<band).astype(F32)*(mp+EPS))
     st=iota((64,128),1)&63
     meas=jnp.where(st<(64>>band),meas*scale,0.0)
     return jnp.where(occ,meas+spart,0.0)
+
+
+EVEN, ODD = pl.ds(0, 128, stride=2), pl.ds(1, 128, stride=2)
+
+
+def rows_of(j, n):
+    return pl.ds(pl.multiple_of(n * j, n), n)
 
 
 def kernel(x_h, cnt_h, edges_h, dyn_h, prev_h, f1h_h, f1l_h, mmh_h, mml_h, w2h_h, w2l_h, tw_h, g_h, pl_h, co_h,
@@ -215,7 +224,7 @@
     bar = pltpu.get_barrier_semaphore()
 
     z16, y2, c1 = me & 112, me & 14, me & 1
-    ys = [((y2 + 2 * d) & 14) | (c1 ^ c) for d in (4, 3, 5, 2, 6, 1, 7, 0) for c in (1, 0)]
+    ys = [((y2 + 2 * d) & 14) | (c1 ^ c) for d in (4, 5, 3, 6, 2, 7, 1, 0) for c in (1, 0)]
 
     def far_first(act):
         def ring(i, c):
@@ -234,12 +243,13 @@
     for ld in loads[1:]:
         ld.start()
     loads[0].wait()
-    s1[...] = jnp.concatenate([jnp.transpose(x_v[0:128, :]), jnp.transpose(x_v[128:256, :])], 1)
+    s1[EVEN, :] = jnp.transpose(x_v[0:128, :])
+    s1[ODD, :] = jnp.transpose(x_v[128:256, :])
     pl.semaphore_wait(bar, ND + 2)
 
-    def send_all(s, r, k):
+    def send_all(s, r, k, n=2):
         def one(j):
-            pltpu.make_async_remote_copy(s.at[pl.ds(j, 1)], r.at[pl.ds(me, 1)], sem.at[k], sem.at[k + 1],
+            pltpu.make_async_remote_copy(s.at[rows_of(j, n)], r.at[rows_of(me, n)], sem.at[k], sem.at[k + 1],
                                          device_id={"bins": j}, device_id_type=MESH).start()
         far_first(one)
 
@@ -248,7 +258,7 @@
         pltpu.make_async_copy(d, d, sem.at[k]).wait()
 
     send_all(s1, r1, 0)
-    r1[pl.ds(me, 1), :] = s1[pl.ds(me, 1), :]
+    r1[rows_of(me, 2), :] = s1[rows_of(me, 2), :]
     for ld in loads[1:]:
         ld.wait()
     T = twiddle(me)
@@ -264,28 +274,29 @@
     wait_all(256, 1)
     wait_all(256, 0)
 
-    s2[...] = stage1(r1[...], (f1h_v[...], f1l_v[...]), (w2h_v[...], w2l_v[...]), tw_v)
+    s2[EVEN, :], s2[ODD, :] = stage1(jnp.concatenate([r1[EVEN, :], r1[ODD, :]], 1), (f1h_v[...], f1l_v[...]), (w2h_v[...], w2l_v[...]), tw_v)
     send_all(s2, r2, 2)
-    r2[pl.ds(me, 1), :] = s2[pl.ds(me, 1), :]
+    r2[rows_of(me, 2), :] = s2[rows_of(me, 2), :]
     wait_all(256, 3)
     wait_all(256, 2)
 
-    Fr, Fi, Qt = stage2(r2[...], me, [t_v[i] for i in range(4)], (mmh_v[...], mml_v[...]), g_v[...])
-    xs[...] = Qt[0:8]
-    xs[1:2, :] = Qt[32:33]
+    sums, y, E = stage2(jnp.concatenate([r2[EVEN, :], r2[ODD, :]], 1), me, [t_v[i] for i in range(4)], (mmh_v[...], mml_v[...]))
+    xs[0:4, :] = sums[0:4, 0:128]
+    xs[4:8, :] = sums[4:8, 128:256]
     for i in range(1, 4):
         pltpu.make_async_remote_copy(xs, xr.at[mx], sem.at[4], sem.at[5],
                                      device_id={"scans": lax.rem(mx + i, 4)}, device_id_type=MESH).start()
     xr[mx] = xs[...]
     S = [oh_v[i] > 0.5 for i in range(3)]
-    mr, mi = stage3(Fr, Fi, S)
+    Fr, Fi = stage2b(y, E, (mmh_v[...], mml_v[...]), g_v[...])
+    mr, mi = stage3(Fr, Fi, E, S)
     mi = pltpu.roll(mi, 64, 1)
     d = xr.at[pl.ds(0, 3)]
     pltpu.make_async_copy(d, d, sem.at[5]).wait()
     pltpu.make_async_copy(d, d, sem.at[4]).wait()
     tot = xr[0] + xr[1] + xr[2] + xr[3]
     s3[...] = stage3b(mr, mi, S, tot)
-    send_all(s3, r3, 6)
+    send_all(s3, r3, 6, 1)
     r3[pl.ds(me, 1), :] = s3[pl.ds(me, 1), :]
     wait_all(128, 7)
     wait_all(128, 6)
@@ -311,7 +322,7 @@
         in_specs=[pl.BlockSpec(memory_space=pltpu.HBM)] * len(ins),
         out_specs=pl.BlockSpec(memory_space=V),
         scratch_shapes=[(pltpu.SMEM if i.shape == (6,) else V)(i.shape, i.dtype) for i in ins] + [
-            *[V((128, 256), F32)] * 4, *[V((128, 128), F32)] * 2, V((8, 128), F32), V((4, 8, 128), F32),
+            *[V((256, 128), F32)] * 4, *[V((128, 128), F32)] * 2, V((8, 128), F32), V((4, 8, 128), F32),
             V((127, 1, 256), F32), V((4, 128, 128), F32), V((3, 128, 128), F32), V((64, 128), F32), V((320, 128), BF),
             pltpu.SemaphoreType.DMA((len(ins),)), pltpu.SemaphoreType.DMA((8,))],
         compiler_params=pltpu.CompilerParams(collective_id=0, has_side_effects=True, vmem_limit_bytes=48 << 20),

time: 44.7 us -> 44.4 us (level)
  no operation moved by 1% of the time
where the time goes in v4:
time: 44.4 us; the launch traced here: 44.3 us
  Pallas kernels  43.7 us (98%)
  local copies, waits for them, and re-layouts  0.62 us (1%)
    pallas_call x1, Pallas kernels, body(): pl.pallas_call(kernel, out_shape=V((64, 128), F32), in_specs=[pl.BlockSpe...  43.7 us

profile of v4, /device:TPU:1, one launch (start us, length us, event | category | flops | bytes accessed | tf_op | source)
XLA Modules:
  0.0 44.3 jit_solution(7269651277942752716)
XLA Ops:
  0.0 43.7 %shard_map.145 = f32[64,128]{1,0:T(8,128)S(1)} custom-call(f32[256,128]{1,0:T(8,128)} %bitcast.7, s32[1,128]{1,0:T(1,128)} %bitcast.9, s32[6]{0:T(128)} %edges_h.1, f32[5,64,64]{2,1,0:T(8,128)} %dyn_h.1, f32[64,128]{1,0:T(8,128)} %bitcast.8, bf16[256,256]{1,0:T(8,128)(2,1)} %constant.20.clone.f1h_h, bf16[256,128]{1,0:T(8,128)(2,1)} %constant.21.clone.f1l_h, ...), custom_call_target="tpu_custom_call" | custom-call | tf_op jit(solution)/shard_map/pallas_call | solution.py:319
  43.7 0.6 %copy.18 = f32[64,1,128]{2,1,0:T(1,128)} copy(f32[64,1,128]{2,1,0:T(1,128)S(1)} %bitcast.6) | data formatting | bytes 65536

commit v5 on v4

--- a/solution.py
+++ b/solution.py
@@ -13,15 +13,22 @@
 BF=jnp.bfloat16; F32=jnp.float32
 ND=128; NB=1<<22; M=1<<15; EPS=1e-5; NCLASS=5
 
-def pair(a):
-    a=np.asarray(a,np.float64)
-    hi=a.astype(np.float32).astype(ml_dtypes.bfloat16)
-    lo=(a-hi.astype(np.float64)).astype(np.float32).astype(ml_dtypes.bfloat16)
-    return hi,lo
+def triple(a):
+    parts=[]
+    for _ in range(3):
+        parts.append(a.astype(np.float32).astype(ml_dtypes.bfloat16))
+        a=a-parts[-1].astype(np.float64)
+    return parts
 def split(x):
     hi=x.astype(BF); lo=(x-hi.astype(F32)).astype(BF)
     return hi,lo
 def dot(a,b): return lax.dot_general(a,b,(((1,),(0,)),((),())),preferred_element_type=F32)
+def split3(x):
+    p=x.astype(BF); r=x-p.astype(F32); q=r.astype(BF)
+    return p,q,(r-q.astype(F32)).astype(BF)
+def dot6(a,b,d=None):
+    d=d or dot
+    return d(a[0],b[0])+((d(a[0],b[1])+d(a[1],b[0]))+((d(a[0],b[2])+d(a[2],b[0]))+d(a[1],b[1])))
 def dot_nt(a,b): return lax.dot_general(a,b,(((1,),(1,)),((),())),preferred_element_type=F32)
 def dot3(a,b,d=dot):
     return d(a[0],b[0])+(d(a[0],b[1])+d(a[1],b[0]))
@@ -56,21 +63,22 @@
         for k in range(64):
             co[be,k,k>>be]=1; co[be,64+k,64+(k>>be)]=1
     co=co.reshape(640,128)
-    f1h,f1l=pair(F1)
-    return dict(F1=(np.concatenate([f1h,f1h],1),f1l),MM=pair(MM),W2=pair(W2),tw=tw,G=np.concatenate([G,G],0).astype(ml_dtypes.bfloat16),place=place.astype(ml_dtypes.bfloat16),co=co.astype(ml_dtypes.bfloat16))
+    f0,f1,f2=triple(F1)
+    return dict(F1=[np.concatenate(f,1) for f in ((f0,f0),(f1,f1),(f0,f2))],MM=triple(MM),W2=triple(W2),tw=tw,G=np.concatenate([G,G],0).astype(ml_dtypes.bfloat16),place=place.astype(ml_dtypes.bfloat16),co=co.astype(ml_dtypes.bfloat16))
 
 def iota(shape,d): return lax.broadcasted_iota(jnp.int32,shape,d)
 
 def stage1(R1, F1, W2, tw):
-    gh,gl=split(R1)
-    A=dot(F1[0],jnp.concatenate([gh,gl],0))+dot(F1[1],gh)
+    g0,g1,g2=split3(R1)
+    g01=jnp.concatenate([g0,g1],0)
+    A=dot(F1[0],g01)+(dot(F1[1],g01)+dot(F1[2],jnp.concatenate([g2,g0],0)))
     Ar,Ai=A[:128],A[128:]
     tr,ti=tw[0],tw[1]
     Br=Ar*tr-Ai*ti; Bi=Ar*ti+Ai*tr
-    (rh,rl),(ih,il)=split(Br),split(Bi)
+    rs,qs=split3(Br),split3(Bi)
     def both(r,i):
         return jnp.concatenate([jnp.concatenate([r,i],1),jnp.concatenate([i,-r],1)],0)
-    Y=dot3(W2, (both(rh,ih),both(rl,il)), dot_nt)
+    Y=dot6(W2, [both(r,i) for r,i in zip(rs,qs)], dot_nt)
     lane=iota((1,256),1)
     nyq=jnp.sum(jnp.where(lane%2==0,Br[0:1],-Br[0:1]),axis=1,keepdims=True)
     first=(iota((128,256),0)==0)&(iota((128,256),1)==128)
@@ -93,19 +101,19 @@
     Yr=Rr*Tr+Ri0*Ts; Yi=Ri0*Tr-Rr*Ts
     Er=jnp.where(zero,Ri*Nr,Yr); Ei=jnp.where(zero,-Ri*Ns,Yi)
     Y=jnp.concatenate([Yr,Yi],0); E=jnp.concatenate([Er,Ei],0)
-    yh,yl=split(Y); eh,el=split(E)
-    X=dot3(MM,(jnp.concatenate([yh,eh],1),jnp.concatenate([yl,el],1)))
+    ys,es=split3(Y),split3(E)
+    X=dot6(MM,[jnp.concatenate([y,e],1) for y,e in zip(ys,es)])
     Xr,Xi,Er,Ei=X[:128,:128],X[128:,:128],X[:128,128:],X[128:,128:]
     rows=iota((128,128),0)
     Pw=jnp.where(lane0&(rows>=64),0.0,Xr*Xr+Xi*Xi)
     Pe=jnp.where(lane0,Er*Er+Ei*Ei,0.0)
     ph,pl_=split(jnp.concatenate([Pw,Pe],0))
     sums=dot_nt(jnp.ones((8,256),BF),jnp.concatenate([ph,pl_],1))
-    return sums,(yh,yl),(Er,Ei)
+    return sums,ys,(Er,Ei)
 
 def stage2b(y, E, MM, G):
-    Z=dot(jnp.concatenate(y,1),G)
-    F=dot3(MM,split(Z))
+    Z=dot(jnp.concatenate(y[:2],1),G)+dot(y[2],G[:128])
+    F=dot6(MM,split3(Z))
     return F[:128],F[128:]
 
 def starts_of(counts_row):
@@ -170,7 +178,7 @@
     out=jnp.zeros((128,64),F32)
     for be in range(NCLASS):
         x=jnp.where(band2==be,pr,0.0)
-        out=out+dot3(split(x),split(dyn[be]),dot_nt)
+        out=out+dot6(split3(x),split3(dyn[be]),dot_nt)
     out=jnp.where(lane<cnt,out,0.0)
     return jnp.concatenate([out[:64],out[64:]],1)
 
@@ -211,14 +219,14 @@
     return pl.ds(pl.multiple_of(n * j, n), n)
 
 
-def kernel(x_h, cnt_h, edges_h, dyn_h, prev_h, f1h_h, f1l_h, mmh_h, mml_h, w2h_h, w2l_h, tw_h, g_h, pl_h, co_h,
+def kernel(x_h, cnt_h, edges_h, dyn_h, prev_h, f1a_h, f1b_h, f1c_h, mma_h, mmb_h, mmc_h, w2a_h, w2b_h, w2c_h, tw_h, g_h, pl_h, co_h,
            o_ref,
-           x_v, cnt_v, edges_v, dyn_v, prev_v, f1h_v, f1l_v, mmh_v, mml_v, w2h_v, w2l_v, tw_v, g_v, pl_v, co_v,
+           x_v, cnt_v, edges_v, dyn_v, prev_v, f1a_v, f1b_v, f1c_v, mma_v, mmb_v, mmc_v, w2a_v, w2b_v, w2c_v, tw_v, g_v, pl_v, co_v,
            s1, r1, s2, r2, s3, r3, xs, xr, dummy, t_v, oh_v, sp_v, sel_v, csem, sem):
     me = lax.axis_index("bins")
     mx = lax.axis_index("scans")
-    hs = [x_h, cnt_h, edges_h, dyn_h, prev_h, f1h_h, f1l_h, mmh_h, mml_h, w2h_h, w2l_h, tw_h, g_h, pl_h, co_h]
-    vs = [x_v, cnt_v, edges_v, dyn_v, prev_v, f1h_v, f1l_v, mmh_v, mml_v, w2h_v, w2l_v, tw_v, g_v, pl_v, co_v]
+    hs = [x_h, cnt_h, edges_h, dyn_h, prev_h, f1a_h, f1b_h, f1c_h, mma_h, mmb_h, mmc_h, w2a_h, w2b_h, w2c_h, tw_h, g_h, pl_h, co_h]
+    vs = [x_v, cnt_v, edges_v, dyn_v, prev_v, f1a_v, f1b_v, f1c_v, mma_v, mmb_v, mmc_v, w2a_v, w2b_v, w2c_v, tw_v, g_v, pl_v, co_v]
     loads = [pltpu.make_async_copy(h, v, csem.at[i]) for i, (h, v) in enumerate(zip(hs, vs))]
     loads[0].start()
     bar = pltpu.get_barrier_semaphore()
@@ -274,13 +282,13 @@
     wait_all(256, 1)
     wait_all(256, 0)
 
-    s2[EVEN, :], s2[ODD, :] = stage1(jnp.concatenate([r1[EVEN, :], r1[ODD, :]], 1), (f1h_v[...], f1l_v[...]), (w2h_v[...], w2l_v[...]), tw_v)
+    s2[EVEN, :], s2[ODD, :] = stage1(jnp.concatenate([r1[EVEN, :], r1[ODD, :]], 1), (f1a_v[...], f1b_v[...], f1c_v[...]), (w2a_v[...], w2b_v[...], w2c_v[...]), tw_v)
     send_all(s2, r2, 2)
     r2[rows_of(me, 2), :] = s2[rows_of(me, 2), :]
     wait_all(256, 3)
     wait_all(256, 2)
 
-    sums, y, E = stage2(jnp.concatenate([r2[EVEN, :], r2[ODD, :]], 1), me, [t_v[i] for i in range(4)], (mmh_v[...], mml_v[...]))
+    sums, y, E = stage2(jnp.concatenate([r2[EVEN, :], r2[ODD, :]], 1), me, [t_v[i] for i in range(4)], (mma_v[...], mmb_v[...], mmc_v[...]))
     xs[0:4, :] = sums[0:4, 0:128]
     xs[4:8, :] = sums[4:8, 128:256]
     for i in range(1, 4):
@@ -288,7 +296,7 @@
                                      device_id={"scans": lax.rem(mx + i, 4)}, device_id_type=MESH).start()
     xr[mx] = xs[...]
     S = [oh_v[i] > 0.5 for i in range(3)]
-    Fr, Fi = stage2b(y, E, (mmh_v[...], mml_v[...]), g_v[...])
+    Fr, Fi = stage2b(y, E, (mma_v[...], mmb_v[...], mmc_v[...]), g_v[...])
     mr, mi = stage3(Fr, Fi, E, S)
     mi = pltpu.roll(mi, 64, 1)
     d = xr.at[pl.ds(0, 3)]

time: 44.4 us -> 45.2 us (1.018)
  Pallas kernels: 43.7 us -> 44.4 us
    pallas_call x1, Pallas kernels: 43.7 us -> 44.4 us  [body(): pl.pallas_call(kernel, out_shape=V((64, 128), F32), in_specs=[pl.BlockSpe...]
where the time goes in v5:
time: 45.2 us; the launch traced here: 45.1 us
  Pallas kernels  44.4 us (98%)
  local copies, waits for them, and re-layouts  0.62 us (1%)
    pallas_call x1, Pallas kernels, body(): pl.pallas_call(kernel, out_shape=V((64, 128), F32), in_specs=[pl.BlockSpe...  44.4 us

profile of v5, /device:TPU:1, one launch (start us, length us, event | category | flops | bytes accessed | tf_op | source)
XLA Modules:
  0.0 45.1 jit_solution(14274278963806631583)
XLA Ops:
  0.0 44.4 %shard_map.172 = f32[64,128]{1,0:T(8,128)S(1)} custom-call(f32[256,128]{1,0:T(8,128)} %bitcast.7, s32[1,128]{1,0:T(1,128)} %bitcast.9, s32[6]{0:T(128)} %edges_h.1, f32[5,64,64]{2,1,0:T(8,128)} %dyn_h.1, f32[64,128]{1,0:T(8,128)} %bitcast.8, bf16[256,256]{1,0:T(8,128)(2,1)} %constant.26.clone.f1a_h, bf16[256,256]{1,0:T(8,128)(2,1)} %constant.27.clone.f1b_h, ...), custom_call_target="tpu_custom_call" | custom-call | tf_op jit(solution)/shard_map/pallas_call | solution.py:327
  44.4 0.6 %copy.21 = f32[64,1,128]{2,1,0:T(1,128)} copy(f32[64,1,128]{2,1,0:T(1,128)S(1)} %bitcast.6) | data formatting | bytes 65536

commit v6 on v5

--- a/solution.py
+++ b/solution.py
@@ -29,6 +29,11 @@
 def dot6(a,b,d=None):
     d=d or dot
     return d(a[0],b[0])+((d(a[0],b[1])+d(a[1],b[0]))+((d(a[0],b[2])+d(a[2],b[0]))+d(a[1],b[1])))
+def dot6s(a,b,d=None):
+    d=d or dot
+    m=a.shape[0]//3
+    p,q,t=d(a,b[0]),d(a[:2*m],b[1]),d(a[:m],b[2])
+    return p[:m]+((q[:m]+p[m:2*m])+((t+p[2*m:])+q[m:]))
 def dot_nt(a,b): return lax.dot_general(a,b,(((1,),(1,)),((),())),preferred_element_type=F32)
 def dot3(a,b,d=dot):
     return d(a[0],b[0])+(d(a[0],b[1])+d(a[1],b[0]))
@@ -64,21 +69,22 @@
             co[be,k,k>>be]=1; co[be,64+k,64+(k>>be)]=1
     co=co.reshape(640,128)
     f0,f1,f2=triple(F1)
-    return dict(F1=[np.concatenate(f,1) for f in ((f0,f0),(f1,f1),(f0,f2))],MM=triple(MM),W2=triple(W2),tw=tw,G=np.concatenate([G,G],0).astype(ml_dtypes.bfloat16),place=place.astype(ml_dtypes.bfloat16),co=co.astype(ml_dtypes.bfloat16))
+    return dict(F1=[np.block([[f0,f0],[f1,f1]]),np.concatenate([f0,f2],1)],MM=np.concatenate(triple(MM),0),W2=np.concatenate(triple(W2),0),tw=tw,G=np.concatenate([G,G],0).astype(ml_dtypes.bfloat16),place=place.astype(ml_dtypes.bfloat16),co=co.astype(ml_dtypes.bfloat16))
 
 def iota(shape,d): return lax.broadcasted_iota(jnp.int32,shape,d)
 
 def stage1(R1, F1, W2, tw):
     g0,g1,g2=split3(R1)
     g01=jnp.concatenate([g0,g1],0)
-    A=dot(F1[0],g01)+(dot(F1[1],g01)+dot(F1[2],jnp.concatenate([g2,g0],0)))
+    A=dot(F1[0],g01)
+    A=A[:256]+(A[256:]+dot(F1[1],jnp.concatenate([g2,g0],0)))
     Ar,Ai=A[:128],A[128:]
     tr,ti=tw[0],tw[1]
     Br=Ar*tr-Ai*ti; Bi=Ar*ti+Ai*tr
     rs,qs=split3(Br),split3(Bi)
     def both(r,i):
         return jnp.concatenate([jnp.concatenate([r,i],1),jnp.concatenate([i,-r],1)],0)
-    Y=dot6(W2, [both(r,i) for r,i in zip(rs,qs)], dot_nt)
+    Y=dot6s(W2, [both(r,i) for r,i in zip(rs,qs)], dot_nt)
     lane=iota((1,256),1)
     nyq=jnp.sum(jnp.where(lane%2==0,Br[0:1],-Br[0:1]),axis=1,keepdims=True)
     first=(iota((128,256),0)==0)&(iota((128,256),1)==128)
@@ -102,7 +108,7 @@
     Er=jnp.where(zero,Ri*Nr,Yr); Ei=jnp.where(zero,-Ri*Ns,Yi)
     Y=jnp.concatenate([Yr,Yi],0); E=jnp.concatenate([Er,Ei],0)
     ys,es=split3(Y),split3(E)
-    X=dot6(MM,[jnp.concatenate([y,e],1) for y,e in zip(ys,es)])
+    X=dot6s(MM,[jnp.concatenate([y,e],1) for y,e in zip(ys,es)])
     Xr,Xi,Er,Ei=X[:128,:128],X[128:,:128],X[:128,128:],X[128:,128:]
     rows=iota((128,128),0)
     Pw=jnp.where(lane0&(rows>=64),0.0,Xr*Xr+Xi*Xi)
@@ -113,7 +119,7 @@
 
 def stage2b(y, E, MM, G):
     Z=dot(jnp.concatenate(y[:2],1),G)+dot(y[2],G[:128])
-    F=dot6(MM,split3(Z))
+    F=dot6s(MM,split3(Z))
     return F[:128],F[128:]
 
 def starts_of(counts_row):
@@ -219,14 +225,14 @@
     return pl.ds(pl.multiple_of(n * j, n), n)
 
 
-def kernel(x_h, cnt_h, edges_h, dyn_h, prev_h, f1a_h, f1b_h, f1c_h, mma_h, mmb_h, mmc_h, w2a_h, w2b_h, w2c_h, tw_h, g_h, pl_h, co_h,
+def kernel(x_h, cnt_h, edges_h, dyn_h, prev_h, f1a_h, f1b_h, mm_h, w2_h, tw_h, g_h, pl_h, co_h,
            o_ref,
-           x_v, cnt_v, edges_v, dyn_v, prev_v, f1a_v, f1b_v, f1c_v, mma_v, mmb_v, mmc_v, w2a_v, w2b_v, w2c_v, tw_v, g_v, pl_v, co_v,
+           x_v, cnt_v, edges_v, dyn_v, prev_v, f1a_v, f1b_v, mm_v, w2_v, tw_v, g_v, pl_v, co_v,
            s1, r1, s2, r2, s3, r3, xs, xr, dummy, t_v, oh_v, sp_v, sel_v, csem, sem):
     me = lax.axis_index("bins")
     mx = lax.axis_index("scans")
-    hs = [x_h, cnt_h, edges_h, dyn_h, prev_h, f1a_h, f1b_h, f1c_h, mma_h, mmb_h, mmc_h, w2a_h, w2b_h, w2c_h, tw_h, g_h, pl_h, co_h]
-    vs = [x_v, cnt_v, edges_v, dyn_v, prev_v, f1a_v, f1b_v, f1c_v, mma_v, mmb_v, mmc_v, w2a_v, w2b_v, w2c_v, tw_v, g_v, pl_v, co_v]
+    hs = [x_h, cnt_h, edges_h, dyn_h, prev_h, f1a_h, f1b_h, mm_h, w2_h, tw_h, g_h, pl_h, co_h]
+    vs = [x_v, cnt_v, edges_v, dyn_v, prev_v, f1a_v, f1b_v, mm_v, w2_v, tw_v, g_v, pl_v, co_v]
     loads = [pltpu.make_async_copy(h, v, csem.at[i]) for i, (h, v) in enumerate(zip(hs, vs))]
     loads[0].start()
     bar = pltpu.get_barrier_semaphore()
@@ -282,13 +288,13 @@
     wait_all(256, 1)
     wait_all(256, 0)
 
-    s2[EVEN, :], s2[ODD, :] = stage1(jnp.concatenate([r1[EVEN, :], r1[ODD, :]], 1), (f1a_v[...], f1b_v[...], f1c_v[...]), (w2a_v[...], w2b_v[...], w2c_v[...]), tw_v)
+    s2[EVEN, :], s2[ODD, :] = stage1(jnp.concatenate([r1[EVEN, :], r1[ODD, :]], 1), (f1a_v[...], f1b_v[...]), w2_v[...], tw_v)
     send_all(s2, r2, 2)
     r2[rows_of(me, 2), :] = s2[rows_of(me, 2), :]
     wait_all(256, 3)
     wait_all(256, 2)
 
-    sums, y, E = stage2(jnp.concatenate([r2[EVEN, :], r2[ODD, :]], 1), me, [t_v[i] for i in range(4)], (mma_v[...], mmb_v[...], mmc_v[...]))
+    sums, y, E = stage2(jnp.concatenate([r2[EVEN, :], r2[ODD, :]], 1), me, [t_v[i] for i in range(4)], mm_v[...])
     xs[0:4, :] = sums[0:4, 0:128]
     xs[4:8, :] = sums[4:8, 128:256]
     for i in range(1, 4):
@@ -296,7 +302,7 @@
                                      device_id={"scans": lax.rem(mx + i, 4)}, device_id_type=MESH).start()
     xr[mx] = xs[...]
     S = [oh_v[i] > 0.5 for i in range(3)]
-    Fr, Fi = stage2b(y, E, (mma_v[...], mmb_v[...], mmc_v[...]), g_v[...])
+    Fr, Fi = stage2b(y, E, mm_v[...], g_v[...])
     mr, mi = stage3(Fr, Fi, E, S)
     mi = pltpu.roll(mi, 64, 1)
     d = xr.at[pl.ds(0, 3)]
@@ -320,7 +326,7 @@
 
 def body(profiles, band_edges, owner_counts, dynamics, prev_state):
     tb = tables()
-    consts = [*tb["F1"], *tb["MM"], *tb["W2"], tb["tw"], tb["G"], tb["place"], tb["co"]]
+    consts = [*tb["F1"], tb["MM"], tb["W2"], tb["tw"], tb["G"], tb["place"], tb["co"]]
     ins = [profiles.reshape(256, 128), owner_counts.reshape(1, 128), band_edges, dynamics, prev_state.reshape(64, 128)]
     ins += [jnp.asarray(c) for c in consts]
     V = pltpu.VMEM

time: 45.2 us -> 44.7 us (0.989)
  no operation moved by 1% of the time
where the time goes in v6:
time: 44.7 us; the launch traced here: 44.6 us
  Pallas kernels  44 us (98%)
  local copies, waits for them, and re-layouts  0.62 us (1%)
    pallas_call x1, Pallas kernels, body(): pl.pallas_call(kernel, out_shape=V((64, 128), F32), in_specs=[pl.BlockSpe...  44 us

profile of v6, /device:TPU:1, one launch (start us, length us, event | category | flops | bytes accessed | tf_op | source)
XLA Modules:
  0.0 44.6 jit_solution(13913047682389952184)
XLA Ops:
  0.0 44.0 %shard_map.127 = f32[64,128]{1,0:T(8,128)S(1)} custom-call(f32[256,128]{1,0:T(8,128)} %bitcast.7, s32[1,128]{1,0:T(1,128)} %bitcast.9, s32[6]{0:T(128)} %edges_h.1, f32[5,64,64]{2,1,0:T(8,128)} %dyn_h.1, f32[64,128]{1,0:T(8,128)} %bitcast.8, bf16[512,256]{1,0:T(8,128)(2,1)} %constant.16.clone.f1a_h, bf16[256,256]{1,0:T(8,128)(2,1)} %constant.17.clone.f1b_h, ...), custom_call_target="tpu_custom_call" | custom-call | tf_op jit(solution)/shard_map/pallas_call | solution.py:333
  44.0 0.6 %copy.16 = f32[64,1,128]{2,1,0:T(1,128)} copy(f32[64,1,128]{2,1,0:T(1,128)S(1)} %bitcast.6) | data formatting | bytes 65536

commit v7 on v6

--- a/solution.py
+++ b/solution.py
@@ -251,9 +251,9 @@
         for y in ys[:-1]:
             act(z16 | y)
 
-    far_first(lambda j: pl.semaphore_signal(bar, inc=1, device_id={"bins": j}, device_id_type=MESH))
     for i in range(1, 4):
         pl.semaphore_signal(bar, inc=1, device_id={"scans": lax.rem(mx + i, 4)}, device_id_type=MESH)
+    far_first(lambda j: pl.semaphore_signal(bar, inc=1, device_id={"bins": j}, device_id_type=MESH))
     for ld in loads[1:]:
         ld.start()
     loads[0].wait()

time: 44.7 us -> 44.8 us (level)
  no operation moved by 1% of the time
where the time goes in v7:
time: 44.8 us; the launch traced here: 44.6 us
  Pallas kernels  44 us (98%)
  local copies, waits for them, and re-layouts  0.62 us (1%)
    pallas_call x1, Pallas kernels, body(): pl.pallas_call(kernel, out_shape=V((64, 128), F32), in_specs=[pl.BlockSpe...  44 us

profile of v7, /device:TPU:1, one launch (start us, length us, event | category | flops | bytes accessed | tf_op | source)
XLA Modules:
  0.0 44.6 jit_solution(17668504108729070967)
XLA Ops:
  0.0 44.0 %shard_map.127 = f32[64,128]{1,0:T(8,128)S(1)} custom-call(f32[256,128]{1,0:T(8,128)} %bitcast.7, s32[1,128]{1,0:T(1,128)} %bitcast.9, s32[6]{0:T(128)} %edges_h.1, f32[5,64,64]{2,1,0:T(8,128)} %dyn_h.1, f32[64,128]{1,0:T(8,128)} %bitcast.8, bf16[512,256]{1,0:T(8,128)(2,1)} %constant.16.clone.f1a_h, bf16[256,256]{1,0:T(8,128)(2,1)} %constant.17.clone.f1b_h, ...), custom_call_target="tpu_custom_call" | custom-call | tf_op jit(solution)/shard_map/pallas_call | solution.py:333
  44.0 0.6 %copy.16 = f32[64,1,128]{2,1,0:T(1,128)} copy(f32[64,1,128]{2,1,0:T(1,128)S(1)} %bitcast.6) | data formatting | bytes 65536
